TPU v7x, 32 devices: a whole 2x2x4 slice. The times are simulated.
32 devices in a mesh: section: 2 (over x), render: 2 (over core), dp: 8 (over z, y).
Axes of the slice: x: 2, y: 2, z: 4, core: 2. Of those that a mesh axis runs over, the one named last changes fastest.
Arguments:
- section_tokens: bfloat16 [2, 8, 256, 2048], P('section', 'dp', 'render'), may hold values from -60 to 60
- w_qkv: bfloat16 [2, 2048, 3072], P('section', 'dp'), may hold values from -0.5 to 0.5
- w_out: bfloat16 [2, 1024, 2048], P('section', 'dp'), may hold values from -0.1875 to 0.1875
- gains: float32 [2, 2048], P('section'), may hold values from 0.25 to 1.75
- cotangent: bfloat16 [8, 256, 2048], P('dp', 'render'), may hold values from -6 to 6
Outputs:
- token_grads: bfloat16 [2, 8, 256, 2048], P('section', 'dp', 'render')
- qkv_grads: float32 [2, 2048, 3072], P('section', 'dp')
- out_grads: float32 [2, 1024, 2048], P('section', 'dp')
- gain_grads: float32 [2, 2048], P('section')
All inputs are finite; a program needn't handle non-finite values.
Results may differ from a plain program's by a relative error of at most 0.02.
Values may be sent and summed in bfloat16 or wider, within the bound.
A program may use at most 192 MiB of HBM per device.

v0:
```python
import jax
import jax.numpy as jnp
from jax import lax
from jax.sharding import PartitionSpec as P

HEADS = 8
HD = 128


NORM_EPSILON = 1e-06


def shifted(block, axis, distance):
    devices = range(lax.axis_size(axis))
    route = [(i - distance, i) for i in devices if i - distance in devices]
    return lax.ppermute(block, axis, route)


def rms_norm(values, gain_row):
    wide_rows = values.astype(jnp.float32)
    row_scale = lax.rsqrt(jnp.mean(wide_rows * wide_rows, axis=-1, keepdims=True) + NORM_EPSILON)
    return ((wide_rows * row_scale * gain_row).astype(jnp.bfloat16), row_scale)


def norm_back(values, row_scale, gain_row, upstream):
    wide_rows = values.astype(jnp.float32)
    grad_wide = upstream.astype(jnp.float32)
    scaled = grad_wide * gain_row
    inner_sum = jnp.sum(scaled * wide_rows, axis=-1, keepdims=True)
    result = row_scale * scaled - wide_rows * row_scale**3 * inner_sum / values.shape[-1]
    gain_term = jnp.sum(grad_wide * wide_rows * row_scale, axis=0)
    return (result, gain_term)


def split_heads(values):
    return values.reshape(values.shape[0], HEADS, HD)


def only_when(flag, compute):

    def skipped():
        return jax.tree.map(jnp.zeros_like, compute())

    return lax.cond(flag, compute, skipped)


def attend(queries, key_rows, value_rows):
    factor = HD ** (-0.5)
    scores = (
        jnp.einsum(
            "qhd,khd->hqk",
            split_heads(queries),
            split_heads(key_rows),
            preferred_element_type=jnp.float32,
        )
        * factor
    )
    row_top = jnp.max(scores, axis=-1, keepdims=True)
    raised = jnp.exp(scores - row_top)
    row_total = jnp.sum(raised, axis=-1, keepdims=True)
    attn_prob = raised / row_total
    mixed_heads = jnp.einsum(
        "hqk,khd->qhd",
        attn_prob.astype(jnp.bfloat16),
        split_heads(value_rows),
        preferred_element_type=jnp.float32,
    )
    return (
        mixed_heads.reshape(queries.shape[0], HEADS * HD).astype(jnp.bfloat16),
        attn_prob,
        row_top,
        row_total,
    )


def score_grad(attn_prob, upstream, value_rows):
    factor = HD ** (-0.5)
    grad_prob = jnp.einsum(
        "qhd,khd->hqk",
        split_heads(upstream),
        split_heads(value_rows),
        preferred_element_type=jnp.float32,
    )
    row_delta = jnp.sum(grad_prob * attn_prob, axis=-1, keepdims=True)
    grad_score = (attn_prob * (grad_prob - row_delta) * factor).astype(jnp.bfloat16)
    return (grad_score, row_delta)


def key_terms_of(grad_score, attn_prob, queries, upstream):
    grad_key = jnp.einsum(
        "hqk,qhd->khd", grad_score, split_heads(queries), preferred_element_type=jnp.float32
    )
    grad_value = jnp.einsum(
        "hqk,qhd->khd",
        attn_prob.astype(jnp.bfloat16),
        split_heads(upstream),
        preferred_element_type=jnp.float32,
    )
    key_count = grad_key.shape[0]
    return (grad_key.reshape(key_count, HEADS * HD), grad_value.reshape(key_count, HEADS * HD))


def shards(section_tokens, w_qkv, w_out, gains, cotangent):
    tokens = section_tokens[0, 0]
    upstream = cotangent[0]
    gain_row = gains[0]
    head_width = HEADS * HD
    half_rows = tokens.shape[0] // 2
    section_index = lax.axis_index("section")
    is_encoder = section_index == 0
    is_decoder = jnp.logical_not(is_encoder)
    render_index = lax.axis_index("render")
    render_count = lax.axis_size("render")
    qkv_cols = w_qkv.shape[2] // render_count
    out_cols = w_out.shape[2] // render_count
    qkv_piece = lax.dynamic_slice_in_dim(w_qkv[0], render_index * qkv_cols, qkv_cols, 1)
    out_piece = lax.dynamic_slice_in_dim(w_out[0], render_index * out_cols, out_cols, 1)
    qkv_piece, out_piece = (
        lax.all_gather(qkv_piece, "dp", axis=0, tiled=True),
        lax.all_gather(out_piece, "dp", axis=0, tiled=True),
    )
    full_qkv, full_out = (
        lax.all_gather(qkv_piece, "render", axis=1, tiled=True),
        lax.all_gather(out_piece, "render", axis=1, tiled=True),
    )
    normed, row_scale = rms_norm(tokens, gain_row)
    projected = jnp.dot(normed, full_qkv, preferred_element_type=jnp.float32).astype(jnp.bfloat16)
    own_kv = projected[:, head_width:]
    enc_query = projected[half_rows:, :head_width]
    all_kv = lax.all_gather(own_kv, "render", axis=0, tiled=True)

    def encoder_forward():
        enc_mixed, enc_prob, enc_top, enc_total = attend(
            enc_query, all_kv[:, :head_width], all_kv[:, head_width:]
        )
        latent = (
            tokens[half_rows:].astype(jnp.float32)
            + jnp.dot(enc_mixed, full_out, preferred_element_type=jnp.float32)
        ).astype(jnp.bfloat16)
        return (enc_mixed, enc_prob, enc_top, enc_total, latent)

    enc_mixed, enc_prob, enc_top, enc_total, latent = only_when(is_encoder, encoder_forward)
    arrived = shifted(latent, "section", 1)

    def latent_project():
        lat_norm, lat_scale = rms_norm(arrived, gain_row)
        lat_kv = jnp.dot(
            lat_norm, full_qkv[:, head_width:], preferred_element_type=jnp.float32
        ).astype(jnp.bfloat16)
        return (lat_norm, lat_scale, lat_kv)

    lat_norm, lat_scale, lat_kv = only_when(is_decoder, latent_project)
    scene_kv = lax.all_gather(lat_kv, "render", axis=0, tiled=True)
    lat_count = scene_kv.shape[0]

    def decoder_attention():
        key_rows = jnp.concatenate(
            [scene_kv[:, :head_width], projected[:, head_width : 2 * head_width]], 0
        )
        value_rows = jnp.concatenate([scene_kv[:, head_width:], projected[:, 2 * head_width :]], 0)
        dec_query = projected[:, :head_width]
        dec_mixed, dec_prob, dec_top, dec_total = attend(dec_query, key_rows, value_rows)
        dec_out_part = jnp.einsum(
            "nc,nd->cd", dec_mixed, upstream, preferred_element_type=jnp.float32
        ).astype(jnp.bfloat16)
        grad_mixed = jnp.einsum(
            "nd,cd->nc", upstream, full_out, preferred_element_type=jnp.float32
        ).astype(jnp.bfloat16)
        dec_score, dec_delta = score_grad(dec_prob, grad_mixed, value_rows)
        dec_grad_query = jnp.einsum(
            "hqk,khd->qhd", dec_score, split_heads(key_rows), preferred_element_type=jnp.float32
        ).reshape(dec_query.shape[0], head_width)
        dec_grad_key, dec_grad_value = key_terms_of(dec_score, dec_prob, dec_query, grad_mixed)
        lat_terms = jnp.concatenate([dec_grad_key[:lat_count], dec_grad_value[:lat_count]], 1)
        dec_grad_proj = jnp.concatenate(
            [dec_grad_query, dec_grad_key[lat_count:], dec_grad_value[lat_count:]], 1
        ).astype(jnp.bfloat16)
        return (lat_terms, dec_grad_proj, dec_out_part)

    lat_terms, dec_grad_proj, dec_out_part = only_when(is_decoder, decoder_attention)
    lat_grad = lax.psum_scatter(
        lat_terms.astype(jnp.bfloat16), "render", scatter_dimension=0, tiled=True
    )

    def decoder_finish():
        dec_qkv_part = jnp.einsum(
            "nd,nc->dc", normed, dec_grad_proj, preferred_element_type=jnp.float32
        )
        lat_weight_part = jnp.einsum(
            "nd,nc->dc", lat_norm, lat_grad, preferred_element_type=jnp.float32
        )
        dec_qkv_part = dec_qkv_part.at[:, head_width:].add(lat_weight_part).astype(jnp.bfloat16)
        grad_normed = jnp.einsum(
            "nc,dc->nd", dec_grad_proj, full_qkv, preferred_element_type=jnp.float32
        ).astype(jnp.bfloat16)
        grad_lat_norm = jnp.einsum(
            "nc,dc->nd", lat_grad, full_qkv[:, head_width:], preferred_element_type=jnp.float32
        ).astype(jnp.bfloat16)
        dec_back, dec_gain_first = norm_back(tokens, row_scale, gain_row, grad_normed)
        dec_result = (upstream.astype(jnp.float32) + dec_back).astype(jnp.bfloat16)
        lat_back, dec_gain_second = norm_back(arrived, lat_scale, gain_row, grad_lat_norm)
        return (
            dec_qkv_part,
            dec_result,
            lat_back.astype(jnp.bfloat16),
            dec_gain_first + dec_gain_second,
        )

    dec_qkv_part, dec_result, lat_back, dec_gain = only_when(is_decoder, decoder_finish)
    returned = shifted(lat_back, "section", -1)

    def encoder_back_start():
        enc_keys = all_kv[:, :head_width]
        enc_values = all_kv[:, head_width:]
        enc_out_part = jnp.einsum(
            "nc,nd->cd", enc_mixed, returned, preferred_element_type=jnp.float32
        ).astype(jnp.bfloat16)
        grad_enc_mixed = jnp.einsum(
            "nd,cd->nc", returned, full_out, preferred_element_type=jnp.float32
        ).astype(jnp.bfloat16)
        enc_score, enc_delta = score_grad(enc_prob, grad_enc_mixed, enc_values)
        query_grad = (
            jnp.einsum(
                "hqk,khd->qhd", enc_score, split_heads(enc_keys), preferred_element_type=jnp.float32
            )
            .reshape(half_rows, head_width)
            .astype(jnp.bfloat16)
        )
        enc_grad_key, enc_grad_value = key_terms_of(enc_score, enc_prob, enc_query, grad_enc_mixed)
        key_terms = jnp.concatenate([enc_grad_key, enc_grad_value], 1)
        return (enc_out_part, grad_enc_mixed, enc_delta, query_grad, key_terms)

    enc_out_part, grad_enc_mixed, enc_delta, query_grad, key_terms = only_when(
        is_encoder, encoder_back_start
    )
    key_grad = lax.psum_scatter(
        key_terms.astype(jnp.bfloat16), "render", scatter_dimension=0, tiled=True
    )

    def encoder_finish():
        query_weight_part = jnp.einsum(
            "nd,nc->dc", normed[half_rows:], query_grad, preferred_element_type=jnp.float32
        )
        key_weight_part = jnp.einsum(
            "nd,nc->dc", normed, key_grad, preferred_element_type=jnp.float32
        )
        enc_qkv_part = jnp.concatenate([query_weight_part, key_weight_part], 1).astype(jnp.bfloat16)
        grad_enc_norm = jnp.einsum(
            "nc,dc->nd", key_grad, full_qkv[:, head_width:], preferred_element_type=jnp.float32
        )
        query_back = jnp.einsum(
            "nc,dc->nd", query_grad, full_qkv[:, :head_width], preferred_element_type=jnp.float32
        )
        grad_enc_norm = grad_enc_norm.at[half_rows:].add(query_back).astype(jnp.bfloat16)
        enc_back, enc_gain_term = norm_back(tokens, row_scale, gain_row, grad_enc_norm)
        enc_result = enc_back.at[half_rows:].add(returned.astype(jnp.float32)).astype(jnp.bfloat16)
        return (enc_qkv_part, enc_result, enc_gain_term)

    enc_qkv_part, enc_result, enc_gain_term = only_when(is_encoder, encoder_finish)
    token_grad = jnp.where(is_encoder, enc_result, dec_result)
    qkv_part = jnp.where(is_encoder, enc_qkv_part, dec_qkv_part).astype(jnp.float32)
    out_part = jnp.where(is_encoder, enc_out_part, dec_out_part).astype(jnp.float32)
    gain_part = jnp.where(is_encoder, enc_gain_term, dec_gain)
    qkv_total, out_total = (
        lax.psum_scatter(
            qkv_part.astype(jnp.bfloat16), "dp", scatter_dimension=0, tiled=True
        ).astype(jnp.float32),
        lax.psum_scatter(
            out_part.astype(jnp.bfloat16), "dp", scatter_dimension=0, tiled=True
        ).astype(jnp.float32),
    )
    qkv_total, out_total = (
        lax.psum(qkv_total.astype(jnp.bfloat16), "render").astype(jnp.float32),
        lax.psum(out_total.astype(jnp.bfloat16), "render").astype(jnp.float32),
    )
    gain_total = lax.psum(gain_part, ("render", "dp"))
    return (token_grad[None, None], qkv_total[None], out_total[None], gain_total[None])


def solution(mesh):
    in_specs = (
        P("section", "dp", "render", None),
        P("section", "dp", None),
        P("section", "dp", None),
        P("section", None),
        P("dp", "render", None),
    )
    out_specs = (
        P("section", "dp", "render", None),
        P("section", "dp", None),
        P("section", "dp", None),
        P("section", None),
    )
    return jax.shard_map(shards, mesh=mesh, in_specs=in_specs, out_specs=out_specs, check_vma=False)
```

profile of v0, /device:TPU:0, one launch (start us, length us, event | category | flops | bytes accessed | tf_op | source)
XLA Modules:
  0.0 723.0 jit_solution(9505677057905056956)
XLA Ops:
  11.3 100.9 %all-gather.12.cloned.1.call-done = bf16[1,2048,1536]{2,1,0:T(8,128)(2,1)} async-done(((bf16[1,256,1536]{2,1,0:T(8,128)(2,1)}), bf16[1,2048,1536]{2,1,0:T(8,128)(2,1)}) %all-gather.12.cloned.1.call-update) | async-done | bytes 6291472 | tf_op jit(solution)/shard_map/all_gather | solution.py:119
  112.3 49.9 %all-gather.16.cloned.1.call-done = bf16[1,1024,1024]{2,1,0:T(8,128)(2,1)} async-done(((bf16[1,128,1024]{2,1,0:T(8,128)(2,1)}), bf16[1,1024,1024]{2,1,0:T(8,128)(2,1)}) %all-gather.16.cloned.1.call-update) | async-done | bytes 2097168 | tf_op jit(solution)/shard_map/all_gather | solution.py:120
  163.2 23.8 %all-gather.14.cloned.1.call-done = bf16[1,2048,3072]{2,1,0:T(8,128)(2,1)} async-done(((bf16[1,2048,1536]{2,1,0:T(8,128)(2,1)}), bf16[1,2048,3072]{2,1,0:T(8,128)(2,1)}) %all-gather.14.cloned.1.call-update) | async-done | bytes 12582928 | tf_op jit(solution)/shard_map/all_gather | solution.py:123
  187.0 6.4 convolution_convert_fusion.11
  194.3 9.0 %all-gather.18.cloned.1.call-done = bf16[1,1024,2048]{2,1,0:T(8,128)(2,1)} async-done(((bf16[1,1024,1024]{2,1,0:T(8,128)(2,1)}), bf16[1,1024,2048]{2,1,0:T(8,128)(2,1)}) %all-gather.18.cloned.1.call-update) | async-done | bytes 4194320 | tf_op jit(solution)/shard_map/all_gather | solution.py:124
  203.3 12.2 %all-gather.10.cloned.1.call-done = bf16[256,2048]{1,0:T(8,128)(2,1)} async-done(((bf16[128,2048]{1,0:T(8,128)(2,1)}), bf16[256,2048]{1,0:T(8,128)(2,1)}) %all-gather.10.cloned.1.call-update) | async-done | bytes 1048592 | tf_op jit(solution)/shard_map/all_gather | solution.py:130
  215.5 10.5 %conditional.6 = (bf16[64,1024]{1,0:T(8,128)(2,1)}, f32[8,64,256]{2,1,0:T(8,128)}, bf16[64,2048]{1,0:T(8,128)(2,1)}) conditional(s32[]{:T(128)} %convert_element_type.152, () %tuple.70, (bf16[64,1024]{1,0:T(8,128)(2,1)S(1)}, bf16[256,2048]{1,0:T(8,128)(2,1)}, bf16[128,2048]{1,0:T(8,128)(2,1)S(1)}, bf16[1024,2048]{1,0:T(8,128)(2,1)}) %tuple.148), branch_computations={%region_1.0_spmd, %region_2.0_spmd} | conditional | flops 336658688 | bytes 12718104 | solution.py:44
  222.2 3.8 fusion.1
  227.5 6.5 collective-permute-done
  242.9 43.5 %reduce-scatter.5.cloned.1.call-done = bf16[64,2048]{1,0:T(8,128)(2,1)} async-done(((bf16[128,2048]{1,0:T(8,128)(2,1)}), bf16[64,2048]{1,0:T(8,128)(2,1)}) %reduce-scatter.5.cloned.1.call-update) | async-done | bytes 262160 | tf_op jit(solution)/shard_map/reduce_scatter | solution.py:181
  286.4 6.4 conditional.9
  286.4 6.1 broadcast.171
  294.7 51.6 %collective-permute-done.1 = bf16[64,2048]{1,0:T(8,128)(2,1)S(1)} collective-permute-done((bf16[64,2048]{1,0:T(8,128)(2,1)}, bf16[64,2048]{1,0:T(8,128)(2,1)S(1)}, u32[]{:S(2)}, u32[]{:S(2)}) %collective-permute-start.1) | collective-permute-done | bytes 262176 | tf_op jit(solution)/shard_map/ppermute | solution.py:16
  346.3 16.4 %conditional.10 = (bf16[1024,2048]{1,0:T(8,128)(2,1)}, bf16[64,1024]{1,0:T(8,128)(2,1)S(1)}, bf16[256,2048]{0,1:T(8,128)(2,1)S(1)}) conditional(s32[]{:T(128)} %convert_element_type.152, () %tuple.69, (bf16[64,1024]{1,0:T(8,128)(2,1)}, bf16[64,2048]{1,0:T(8,128)(2,1)S(1)}, bf16[1024,2048]{1,0:T(8,128)(2,1)}, bf16[256,2048]{1,0:T(8,128)(2,1)}, ...), branch_computations={%region_20.21_spmd, %region_21.23_spmd} | conditional | flops 676857344 | bytes 22020148 | solution.py:44
  346.6 4.2 convolution_convert_fusion.6
  364.3 4.7 broadcast_select_fusion.1
  372.8 47.4 %conditional.11 = (bf16[128,2048]{1,0:T(8,128)(2,1)S(1)}, f32[2048]{0:T(1024)S(1)}, bf16[2048,3072]{1,0:T(8,128)(2,1)}) conditional(s32[]{:T(128)} %convert_element_type.152, () %tuple.68, (bf16[128,2048]{1,0:T(8,128)(2,1)S(1)}, bf16[64,1024]{1,0:T(8,128)(2,1)S(1)}, bf16[128,2048]{1,0:T(8,128)(2,1)}, f32[128,1]{0,1:T(1,128)S(1)}, ...), branch_computations={%region_24.0_spmd, %region_25.28_spmd} | conditional | flops 2721183744 | bytes 88929896 | solution.py:44
  372.8 6.4 fusion.94
  388.8 14.6 %pad_maximum_fusion.5 = bf16[2048,3072]{0,1:T(8,128)(2,1)} fusion(bf16[2048,2048]{0,1:T(8,128)(2,1)S(1)} %convolution_convert_fusion.9, bf16[2048,1024]{0,1:T(8,128)(2,1)S(1)} %convolution_convert_fusion.10), kind=kLoop, calls=%fused_computation.123 | loop fusion | flops 25165824 | bytes 25165824 | tf_op jit(solution)/shard_map/cond/branch_1_fun/concatenate | solution.py:247
  403.4 16.8 %copy.100 = bf16[2048,3072]{1,0:T(8,128)(2,1)} copy(bf16[2048,3072]{0,1:T(8,128)(2,1)} %pad_maximum_fusion.5) | data formatting | bytes 25165824 | tf_op jit(solution)/shard_map/cond | solution.py:44
  420.1 10.8 %broadcast_select_fusion = bf16[2048,3072]{1,0:T(8,128)(2,1)} fusion(bf16[2048,3072]{1,0:T(8,128)(2,1)} %get-tuple-element.247, bf16[2048,3072]{1,0:T(8,128)(2,1)} %get-tuple-element.181, pred[]{:T(512)S(6)} %eq.3), kind=kLoop, calls=%fused_computation.148 | loop fusion | flops 6291456 | bytes 37748736 | tf_op jit(solution)/shard_map/jit(_where)/select_n | solution.py:261
  431.0 34.9 %reduce-scatter.11.cloned.1.call-done = bf16[128,2048]{1,0:T(8,128)(2,1)} async-done(((bf16[1024,2048]{1,0:T(8,128)(2,1)}), bf16[128,2048]{1,0:T(8,128)(2,1)}) %reduce-scatter.11.cloned.1.call-update) | async-done | bytes 524304 | tf_op jit(solution)/shard_map/reduce_scatter | solution.py:268
  465.9 210.7 %reduce-scatter.9.cloned.1.call-done = bf16[256,3072]{1,0:T(8,128)(2,1)} async-done(((bf16[2048,3072]{1,0:T(8,128)(2,1)}), bf16[256,3072]{1,0:T(8,128)(2,1)}) %reduce-scatter.9.cloned.1.call-update) | async-done | bytes 1572880 | tf_op jit(solution)/shard_map/reduce_scatter | solution.py:265
  676.6 32.6 %psum.23 = f32[1,2048]{1,0:T(1,128)} all-reduce(f32[1,2048]{1,0:T(1,128)S(1)} %bitcast.198), channel_id=1, replica_groups=mesh['section'=2,'render'=2,'dp'=8] {'render','dp'}, use_global_device_ids=true, to_apply=%region_32.33 | all-reduce | flops 2048 | bytes 16384 | tf_op jit(solution)/shard_map/psum | solution.py:276
  (96 shorter events, 62.5 us)
Async XLA Ops:
  7.2 1.4 copy-start
  7.2 155.1 %copy-start.2 = (bf16[1,1,128,2048]{3,2,1,0:T(8,128)(2,1)S(1)}, bf16[1,1,128,2048]{3,2,1,0:T(8,128)(2,1)}, u32[]{:S(2)}) copy-start(bf16[1,1,128,2048]{3,2,1,0:T(8,128)(2,1)} %param.23) | copy-start | bytes 1572868
  7.2 155.8 %copy-start.9 = (f32[1,2048]{1,0:T(1,128)S(1)}, f32[1,2048]{1,0:T(1,128)}, u32[]{:S(2)}) copy-start(f32[1,2048]{1,0:T(1,128)} %param.26) | copy-start | bytes 24580
  7.2 105.0 %all-gather.12.cloned.1.call-start = ((), (), s32[]{:S(2)}) async-start(), calls=%async_computation.9 | async-start | bytes 7077888 | tf_op jit(solution)/shard_map/all_gather | solution.py:119
  9.5 152.7 %all-gather.16.cloned.1.call-start = ((), (), s32[]{:S(2)}) async-start(), calls=%async_computation.11 | async-start | bytes 2359296 | tf_op jit(solution)/shard_map/all_gather | solution.py:120
  11.3 175.7 %all-gather.14.cloned.1.call-start = ((), (), s32[]{:S(2)}) async-start(), calls=%async_computation.10 | async-start | bytes 18874368 | tf_op jit(solution)/shard_map/all_gather | solution.py:123
  112.2 91.0 %all-gather.18.cloned.1.call-start = ((), (), s32[]{:S(2)}) async-start(), calls=%async_computation.12 | async-start | bytes 6291456 | tf_op jit(solution)/shard_map/all_gather | solution.py:124
  162.2 53.2 %all-gather.10.cloned.1.call-start = ((), (), s32[]{:S(2)}) async-start(), calls=%async_computation.4 | async-start | bytes 1572864 | tf_op jit(solution)/shard_map/all_gather | solution.py:130
  194.2 92.1 %reduce-scatter.5.cloned.1.call-start = ((), (), s32[]{:S(2)}) async-start(), calls=%async_computation.5 | async-start | bytes 786432 | tf_op jit(solution)/shard_map/reduce_scatter | solution.py:181
  226.0 11.1 %copy-start.3 = (bf16[1,128,2048]{2,1,0:T(8,128)(2,1)S(1)}, bf16[1,128,2048]{2,1,0:T(8,128)(2,1)}, u32[]{:S(2)}) copy-start(bf16[1,128,2048]{2,1,0:T(8,128)(2,1)} %param.27) | copy-start | bytes 1572868
  226.0 7.9 %collective-permute-start = (bf16[64,2048]{1,0:T(8,128)(2,1)}, bf16[64,2048]{1,0:T(8,128)(2,1)S(1)}, u32[]{:S(2)}, u32[]{:S(2)}) collective-permute-start(bf16[64,2048]{1,0:T(8,128)(2,1)} %get-tuple-element.168), channel_id=1, source_target_pairs={{0,16},{1,17},{2,18},{3,19},{4,20},{5,21},{6,22},{7,23},{8,24},{9,... | collective-permute-start | bytes 786440 | tf_op jit(solution)/shard_map/ppermute | solution.py:16
  234.8 2.3 copy-start.16
  242.8 129.9 %reduce-scatter.7.cloned.1.call-start = ((), (), s32[]{:S(2)}) async-start(), calls=%async_computation.6 | async-start | bytes 1572864 | tf_op jit(solution)/shard_map/reduce_scatter | solution.py:236
  292.7 0.7 copy-start.11
  293.4 52.9 %collective-permute-start.1 = (bf16[64,2048]{1,0:T(8,128)(2,1)}, bf16[64,2048]{1,0:T(8,128)(2,1)S(1)}, u32[]{:S(2)}, u32[]{:S(2)}) collective-permute-start(bf16[64,2048]{1,0:T(8,128)(2,1)} %copy-done.11), channel_id=1, source_target_pairs={{16,0},{17,1},{18,2},{19,3},{20,4},{21,5},{22,6},{23,7},{24,8},{25... | collective-permute-start | bytes 786440 | tf_op jit(solution)/shard_map/ppermute | solution.py:16
  346.6 9.6 %copy-start.7 = (bf16[64,1024]{1,0:T(8,128)(2,1)}, bf16[64,1024]{1,0:T(8,128)(2,1)S(1)}, u32[]{:S(2)}) copy-start(bf16[64,1024]{1,0:T(8,128)(2,1)S(1)} %get-tuple-element.135) | copy-start | bytes 393220 | tf_op jit(solution)/shard_map/cond
  364.2 101.7 %reduce-scatter.11.cloned.1.call-start = ((), (), s32[]{:S(2)}) async-start(), calls=%async_computation.8 | async-start | bytes 4718592 | tf_op jit(solution)/shard_map/reduce_scatter | solution.py:268
  364.3 8.5 %copy-start.13 = (f32[128,1]{0,1:T(1,128)S(1)}, f32[128,1]{0,1:T(1,128)}, u32[]{:S(2)}) copy-start(f32[128,1]{0,1:T(1,128)} %get-tuple-element.279) | copy-start | bytes 1540
  369.0 307.6 %reduce-scatter.9.cloned.1.call-start = ((), (), s32[]{:S(2)}) async-start(), calls=%async_computation.7 | async-start | bytes 14155776 | tf_op jit(solution)/shard_map/reduce_scatter | solution.py:265
  372.8 11.0 %copy-start.15 = (f32[128,1]{0,1:T(1,128)}, f32[128,1]{0,1:T(1,128)S(1)}, u32[]{:S(2)}) copy-start(f32[128,1]{0,1:T(1,128)S(1)} %get-tuple-element.139) | copy-start | bytes 1540 | tf_op jit(solution)/shard_map/cond
  379.2 5.9 copy-start.6
  403.3 16.8 %copy-start.12 = (f32[2048]{0:T(1024)S(1)}, f32[2048]{0:T(1024)}, u32[]{:S(2)}) copy-start(f32[2048]{0:T(1024)} %get-tuple-element.317) | copy-start | bytes 24580 | tf_op jit(solution)/shard_map/cond
  430.9 284.8 %copy-start.1 = (bf16[1,256,3072]{2,1,0:T(8,128)(2,1)S(1)}, bf16[1,256,3072]{2,1,0:T(8,128)(2,1)}, u32[]{:S(2)}) copy-start(bf16[1,256,3072]{2,1,0:T(8,128)(2,1)} %param.24) | copy-start | bytes 4718596
  431.0 279.2 %all-reduce.3.cloned.1.call-start = ((), (), s32[]{:S(2)}) async-start(), calls=%async_computation.13 | async-start | bytes 4194304 | tf_op jit(solution)/shard_map/psum | solution.py:273
Sparse Core Ops, SparseCore 0:
  10.8 101.4 all-gather.11
  114.9 47.2 all-gather.15
  163.8 23.1 all-gather.13
  188.4 14.8 all-gather.17
  205.2 10.1 all-gather.9
  242.9 43.3 reduce-scatter.4
  364.3 8.3 reduce-scatter.6
  376.4 89.4 reduce-scatter.10
  469.5 207.0 reduce-scatter.8
  678.8 20.5 all-reduce.2
where the time goes:
time: 729 us; the launch traced here: 723 us
  waiting for transfers between devices  547 us (75%)
  other arithmetic  41.6 us (6%)
  local copies, waits for them, and re-layouts  40.8 us (6%)
  matrix products  40.2 us (6%)
  blocking collectives  34.9 us (5%)
  between operations  14.8 us (2%)
    reduce_scatter x1, waiting for transfers between devices, shards(): lax.psum_scatter(qkv_part.astype(jnp.bfloat16), 'dp', scatter_dimension=0...  211 us
    all_gather x1, waiting for transfers between devices, shards(): lax.all_gather(qkv_piece, 'dp', axis=0, tiled=True)  101 us
    ppermute x2, waiting for transfers between devices, shifted(): return lax.ppermute(block, axis, route)  58.1 us
    all_gather x1, waiting for transfers between devices, shards(): lax.all_gather(out_piece, 'dp', axis=0, tiled=True)  49.9 us
    reduce_scatter x1, waiting for transfers between devices, shards(): lax.psum_scatter(lat_terms.astype(jnp.bfloat16), 'render', scatter_dimens...  43.5 us
    reduce_scatter x1, waiting for transfers between devices, shards(): lax.psum_scatter(out_part.astype(jnp.bfloat16), 'dp', scatter_dimension=0...  34.9 us
    psum x1, blocking collectives, shards(): gain_total = lax.psum(gain_part, ('render', 'dp'))  32.6 us
    all_gather x1, waiting for transfers between devices, shards(): lax.all_gather(qkv_piece, 'render', axis=1, tiled=True)  23.8 us
  transfers between devices with their start and end apart: 12, of which 11 were waited for; matrix products, arithmetic and copies ran while one was open for 10% of the time, Pallas kernels for 0%

commit v1 on v0

v1 whole, which is shorter than its diff:
```python
import functools

import jax
import jax.numpy as jnp
from jax import lax
from jax.experimental import pallas as pl
from jax.experimental.pallas import tpu as pltpu
from jax.sharding import PartitionSpec as P

HEADS = 8
HD = 128
NORM_EPSILON = 1e-06
BF = jnp.bfloat16
F32 = jnp.float32
MESH = pl.DeviceIdType.MESH
VMEM = pl.BlockSpec(memory_space=pltpu.VMEM)
ANY = pl.BlockSpec(memory_space=pl.ANY)


def dims():
    return lax.axis_size("dp"), lax.axis_size("render")


def ring_index(pos, n):
    return jnp.where(pos < n // 2, 2 * pos, 2 * (n - 1 - pos) + 1)


def ring_position(index, n):
    return jnp.where(index % 2 == 0, index // 2, n - 1 - index // 2)


def pieces_of(out_rows):
    return max(1, min(4, out_rows // 32))


def rows_at(start, size):
    return pl.ds(pl.multiple_of(start, 8), size)


def signal(**where):
    pl.semaphore_signal(
        pltpu.get_barrier_semaphore(), inc=1, device_id=where, device_id_type=MESH
    )


def remote(src, dst, send, recv, **where):
    return pltpu.make_async_remote_copy(
        src_ref=src, dst_ref=dst, send_sem=send, recv_sem=recv,
        device_id=where, device_id_type=MESH,
    )


def call(body, collective_id, outs, in_specs, out_specs, scratch, limit, args):
    return pl.pallas_call(
        body,
        out_shape=outs,
        in_specs=in_specs,
        out_specs=out_specs,
        scratch_shapes=scratch,
        compiler_params=pltpu.CompilerParams(
            collective_id=collective_id, has_side_effects=True, vmem_limit_bytes=limit << 20
        ),
    )(*args)


def gather_kernel(n, count, qw, ow, tok, cot, qfull, ofull, tfull, cfull,
                  local, qsend, qrecv, osend, orecv, tsend, trecv):
    me = lax.axis_index("dp")
    r = lax.axis_index("render")
    pos = ring_position(me, n)
    hop = [ring_index((pos + 1) % n, n), ring_index((pos + n - 1) % n, n)]
    per = n // count
    q_rows, o_rows = qw.shape[0], ow.shape[0]
    pieces = pieces_of(o_rows)
    qr, orr = q_rows // (2 * pieces), o_rows // (2 * pieces)
    t_rows = tok.shape[0]
    for where in hop:
        signal(dp=where)
    for j in range(1, count):
        signal(render=(r + j) % count)
    pl.semaphore_wait(pltpu.get_barrier_semaphore(), 1 + count)

    def q_at(ref, shard, d, k):
        return ref.at[rows_at(shard * q_rows + (d * pieces + k) * qr, qr)]

    def o_at(ref, shard, d, k):
        return ref.at[rows_at((shard % per) * o_rows + (d * pieces + k) * orr, orr)]

    own_out = me // per == r
    keep = [
        pltpu.make_async_copy(qw, qfull.at[rows_at(me * q_rows, q_rows)], local.at[0]),
        pltpu.make_async_copy(tok, tfull.at[rows_at(r * t_rows, t_rows)], local.at[2]),
        pltpu.make_async_copy(cot, cfull.at[rows_at(r * t_rows, t_rows)], local.at[3]),
    ]
    keep_out = pltpu.make_async_copy(
        ow, ofull.at[rows_at((me % per) * o_rows, o_rows)], local.at[1]
    )

    def token_copies(j, sender):
        where = rows_at(sender * t_rows, t_rows)
        peer = (r + j) % count
        return [
            remote(tok, tfull.at[where], tsend.at[0, j], trecv.at[0, j], render=peer),
            remote(cot, cfull.at[where], tsend.at[1, j], trecv.at[1, j], render=peer),
        ]

    for j in range(1, count):
        for c in token_copies(j, r):
            c.start()

    for d in range(2):
        for k in range(pieces):
            remote(qw.at[pl.ds((d * pieces + k) * qr, qr)], q_at(qfull, me, d, k),
                   qsend.at[d, 0, k], qrecv.at[d, 0, k], dp=hop[d]).start()

            @pl.when(own_out)
            def _():
                remote(ow.at[pl.ds((d * pieces + k) * orr, orr)], o_at(ofull, me, d, k),
                       osend.at[d, 0, k], orecv.at[d, 0, k], dp=hop[d]).start()

    for c in keep:
        c.start()

    @pl.when(own_out)
    def _():
        keep_out.start()

    def shard_at(d, s):
        return ring_index((pos + n - s) % n if d == 0 else (pos + s) % n, n)

    def q_copy(d, s, k, shard):
        ref = q_at(qfull, shard, d, k)
        return remote(ref, ref, qsend.at[d, s, k], qrecv.at[d, s, k], dp=hop[d])

    def o_copy(d, s, k, shard):
        ref = o_at(ofull, shard, d, k)
        return remote(ref, ref, osend.at[d, s, k], orecv.at[d, s, k], dp=hop[d])

    def step(s, last):
        for k in range(pieces):
            for d in range(2):
                shard = shard_at(d, s)
                q_copy(d, s - 1, k, shard).wait_recv()
                if not last:
                    q_copy(d, s, k, shard).start()

                @pl.when(shard // per == r)
                def _():
                    o_copy(d, s - 1, k, shard).wait_recv()
                    if not last:
                        o_copy(d, s, k, shard).start()

    @pl.loop(1, n - 1)
    def _(s):
        step(s, False)

    step(n - 1, True)

    @pl.loop(0, n - 1)
    def _(s):
        for k in range(pieces):
            for d in range(2):
                shard = shard_at(d, s)
                q_copy(d, s, k, shard).wait_send()

                @pl.when(shard // per == r)
                def _():
                    o_copy(d, s, k, shard).wait_send()

    for c in keep:
        c.wait()

    @pl.when(own_out)
    def _():
        keep_out.wait()

    for j in range(1, count):
        for c in token_copies(j, (r + count - j) % count):
            c.wait_send()
            c.wait_recv()


def gather(qw, ow, tok, cot):
    n, count = dims()
    pieces = pieces_of(ow.shape[0])
    sem = lambda *shape: pltpu.SemaphoreType.DMA(shape)
    shape = lambda rows, like: jax.ShapeDtypeStruct((rows, like.shape[1]), BF)
    ring = (2, n - 1, pieces)
    return call(
        functools.partial(gather_kernel, n, count), 0,
        (shape(n * qw.shape[0], qw), shape(n // count * ow.shape[0], ow),
         shape(count * tok.shape[0], tok), shape(count * cot.shape[0], cot)),
        [ANY] * 4, (ANY,) * 4,
        [sem(4), sem(*ring), sem(*ring), sem(*ring), sem(*ring), sem(2, count), sem(2, count)],
        16, (qw, ow, tok, cot),
    )


def hop_kernel(source, back, count, part, base, gain, full, gain_out, own, got,
               psend, precv, xsend, xrecv, fsend, frecv):
    r = lax.axis_index("render")
    section = lax.axis_index("section")
    rows = part.shape[0] // count
    for j in range(1, count):
        signal(render=(r + j) % count)
    signal(section=1 - section)
    pl.semaphore_wait(pltpu.get_barrier_semaphore(), count)
    mine = rows_at(r * rows, rows)
    if back:
        gain_out[...] = jnp.zeros_like(gain_out)

    def across():
        return remote(own, full.at[mine], xsend, xrecv, section=1 - source)

    @pl.when(section == source)
    def _():
        def partial(j):
            peer = (r + j) % count
            return remote(part.at[rows_at(peer * rows, rows)], got.at[j - 1],
                          psend.at[j - 1], precv.at[j - 1], render=peer)

        for j in range(1, count):
            partial(j).start()
        total = part[mine].astype(F32)
        for j in range(1, count):
            partial(j).wait_recv()
            total = total + got[j - 1].astype(F32)
        if back:
            grad = total.astype(BF).astype(F32)
            wide = base[mine].astype(F32)
            scale = lax.rsqrt(jnp.mean(wide * wide, axis=-1, keepdims=True) + NORM_EPSILON)
            scaled = grad * gain[...]
            inner = jnp.sum(scaled * wide, axis=-1, keepdims=True)
            own[...] = (
                scale * scaled - wide * (scale**3 * inner / base.shape[-1])
            ).astype(BF)
            gain_out[...] = jnp.sum(grad * wide * scale, axis=0, keepdims=True)
        else:
            own[...] = (base[...].astype(F32) + total).astype(BF)
        across().start()
        across().wait_send()
        for j in range(1, count):
            partial(j).wait_send()
        full[...] = jnp.zeros_like(full)

    @pl.when(section != source)
    def _():
        across().wait_recv()

        def forward(j, sender):
            ref = full.at[rows_at(sender * rows, rows)]
            return remote(ref, ref, fsend.at[j - 1], frecv.at[j - 1], render=(r + j) % count)

        for j in range(1, count):
            forward(j, r).start()
        for j in range(1, count):
            forward(j, r).wait_send()
            forward(j, (r + count - j) % count).wait_recv()


def section_hop(source, back, part, base, gain):
    _, count = dims()
    rows = part.shape[0] // count
    sem = lambda *shape: pltpu.SemaphoreType.DMA(shape)
    return call(
        functools.partial(hop_kernel, source, back, count), 2 if back else 1,
        (jax.ShapeDtypeStruct(part.shape, BF), jax.ShapeDtypeStruct(gain.shape, F32)),
        [VMEM] * 3, (VMEM, VMEM),
        [pltpu.VMEM((rows, part.shape[1]), BF),
         pltpu.VMEM((count - 1, rows, part.shape[1]), BF),
         sem(count - 1), sem(count - 1), pltpu.SemaphoreType.DMA, pltpu.SemaphoreType.DMA,
         sem(count - 1), sem(count - 1)],
        24, (part, base, gain),
    )


def reduce_kernel(n, count, qpart, opart, dpart, tok, resid, gain, gain_lat,
                  qout, oout, tout, gout, qbuf, obuf, dbuf, gbuf, own_gain,
                  qsend, qrecv, osend, orecv, dsend, drecv, gsend, grecv, fsend, frecv, hsend, hrecv):
    me = lax.axis_index("dp")
    r = lax.axis_index("render")
    pos = ring_position(me, n)
    hop = [ring_index((pos + 1) % n, n), ring_index((pos + n - 1) % n, n)]
    per = n // count
    q_rows, o_rows = qpart.shape[0] // n, opart.shape[0] // per
    pieces = pieces_of(o_rows)
    qr, orr = q_rows // (2 * pieces), o_rows // (2 * pieces)
    t_rows = tok.shape[0]
    everyone = n * count
    flat = me * count + r

    @pl.loop(1, everyone)
    def _(j):
        other = (flat + j) % everyone
        signal(dp=other // count, render=other % count)

    pl.semaphore_wait(pltpu.get_barrier_semaphore(), everyone - 1)

    def q_rows_of(shard, d, k):
        return rows_at(shard * q_rows + (d * pieces + k) * qr, qr)

    def o_rows_of(shard, d, k):
        return rows_at((shard % per) * o_rows + (d * pieces + k) * orr, orr)

    def shard_at(d, s):
        return ring_index((pos + 2 * n - 1 - s) % n if d == 0 else (pos + 1 + s) % n, n)

    def q_copy(src, d, s, k):
        return remote(src, qbuf.at[d, s, k], qsend.at[d, s, k], qrecv.at[d, s, k], dp=hop[d])

    def o_copy(src, d, s, k):
        return remote(src, obuf.at[d, s, k], osend.at[d, s, k], orecv.at[d, s, k], dp=hop[d])

    def block(j):
        peer = (r + j) % count
        return remote(dpart.at[rows_at(peer * t_rows, t_rows)], dbuf.at[j - 1],
                      dsend.at[j - 1], drecv.at[j - 1], render=peer)

    for j in range(1, count):
        block(j).start()

    def first(d, k, shard):
        return q_copy(qpart.at[q_rows_of(shard, d, k)], d, 0, k)

    def first_out(d, k, shard):
        return o_copy(opart.at[o_rows_of(shard, d, k)], d, 0, k)

    for k in range(pieces):
        for d in range(2):
            shard = shard_at(d, 0)
            first(d, k, shard).start()

            @pl.when(shard // per == r)
            def _():
                first_out(d, k, shard).start()

    total = dpart[rows_at(r * t_rows, t_rows)].astype(F32)
    for j in range(1, count):
        block(j).wait_recv()
        total = total + dbuf[j - 1].astype(F32)
    grad = total.astype(BF).astype(F32)
    wide = tok[...].astype(F32)
    scale = lax.rsqrt(jnp.mean(wide * wide, axis=-1, keepdims=True) + NORM_EPSILON)
    scaled = grad * gain[...]
    inner = jnp.sum(scaled * wide, axis=-1, keepdims=True)
    tout[...] = (
        resid[...].astype(F32) + scale * scaled - wide * (scale**3 * inner / tok.shape[-1])
    ).astype(BF)
    own_gain[...] = gain_lat[...] + jnp.sum(grad * wide * scale, axis=0, keepdims=True)

    def gain_copy(j, sender):
        other = (flat + j) % everyone
        return remote(own_gain, gbuf.at[sender], gsend.at[j], grecv.at[j],
                      dp=other // count, render=other % count)

    @pl.loop(1, everyone)
    def _(j):
        gain_copy(j, flat).start()

    @pl.loop(1, n - 1)
    def _(s):
        for k in range(pieces):
            for d in range(2):
                shard = shard_at(d, s)
                held = qbuf.at[d, s - 1, k]
                q_copy(held, d, s - 1, k).wait_recv()
                held[...] = (
                    held[...].astype(F32) + qpart[q_rows_of(shard, d, k)].astype(F32)
                ).astype(BF)
                q_copy(held, d, s, k).start()

                @pl.when(shard // per == r)
                def _():
                    held_out = obuf.at[d, s - 1, k]
                    o_copy(held_out, d, s - 1, k).wait_recv()
                    held_out[...] = (
                        held_out[...].astype(F32) + opart[o_rows_of(shard, d, k)].astype(F32)
                    ).astype(BF)
                    o_copy(held_out, d, s, k).start()

    own_out = me // per == r

    def q_final(j, d, k, sender):
        ref = qout.at[sender, pl.ds((d * pieces + k) * qr, qr)]
        return remote(ref, ref, fsend.at[j - 1, d, k], frecv.at[j - 1, d, k],
                      render=(r + j) % count)

    def o_final(j, d, k):
        ref = oout.at[pl.ds((d * pieces + k) * orr, orr)]
        return remote(ref, ref, hsend.at[j - 1, d, k], hrecv.at[d, k], render=(r + j) % count)

    for k in range(pieces):
        for d in range(2):
            held = qbuf.at[d, n - 2, k]
            q_copy(held, d, n - 2, k).wait_recv()
            qout[r, pl.ds((d * pieces + k) * qr, qr)] = (
                held[...].astype(F32) + qpart[q_rows_of(me, d, k)].astype(F32)
            ).astype(BF)
            for j in range(1, count):
                q_final(j, d, k, r).start()

            @pl.when(own_out)
            def _():
                held_out = obuf.at[d, n - 2, k]
                o_copy(held_out, d, n - 2, k).wait_recv()
                oout[pl.ds((d * pieces + k) * orr, orr)] = (
                    held_out[...].astype(F32) + opart[o_rows_of(me, d, k)].astype(F32)
                ).astype(BF)
                for j in range(1, count):
                    o_final(j, d, k).start()

    sums = own_gain[...]
    gbuf[flat] = sums

    @pl.loop(1, everyone)
    def _(j):
        gain_copy(j, (flat + everyone - j) % everyone).wait_recv()
        gain_copy(j, flat).wait_send()

    gout[...] = jnp.sum(gbuf[...], axis=0)

    @pl.loop(0, n - 1)
    def _(s):
        for k in range(pieces):
            for d in range(2):
                shard = shard_at(d, s)
                q_copy(qbuf.at[d, s, k], d, s, k).wait_send()

                @pl.when(shard // per == r)
                def _():
                    o_copy(obuf.at[d, s, k], d, s, k).wait_send()

    for j in range(1, count):
        block(j).wait_send()
        for k in range(pieces):
            for d in range(2):
                q_final(j, d, k, r).wait_send()
                q_final(j, d, k, (r + count - j) % count).wait_recv()

                @pl.when(own_out)
                def _():
                    o_final(j, d, k).wait_send()

    @pl.when(jnp.logical_not(own_out))
    def _():
        for k in range(pieces):
            for d in range(2):
                o_final(1, d, k).wait_recv()


def reduce_all(qpart, opart, dpart, tok, resid, gain, gain_lat):
    n, count = dims()
    per = n // count
    q_rows, o_rows = qpart.shape[0] // n, opart.shape[0] // per
    pieces = pieces_of(o_rows)
    qr, orr = q_rows // (2 * pieces), o_rows // (2 * pieces)
    sem = lambda *shape: pltpu.SemaphoreType.DMA(shape)
    ring = (2, n - 1, pieces)
    return call(
        functools.partial(reduce_kernel, n, count), 3,
        (jax.ShapeDtypeStruct((count, q_rows, qpart.shape[1]), BF),
         jax.ShapeDtypeStruct((o_rows, opart.shape[1]), BF),
         jax.ShapeDtypeStruct(tok.shape, BF),
         jax.ShapeDtypeStruct(gain.shape, F32)),
        [VMEM] * 7, (VMEM,) * 4,
        [pltpu.VMEM(ring + (qr, qpart.shape[1]), BF),
         pltpu.VMEM(ring + (orr, opart.shape[1]), BF),
         pltpu.VMEM((count - 1,) + tok.shape, BF),
         pltpu.VMEM((n * count,) + gain.shape, F32),
         pltpu.VMEM(gain.shape, F32),
         sem(*ring), sem(*ring), sem(*ring), sem(*ring),
         sem(count - 1), sem(count - 1), sem(n * count), sem(n * count),
         sem(count - 1, 2, pieces), sem(count - 1, 2, pieces),
         sem(count - 1, 2, pieces), sem(2, pieces)],
        40, (qpart, opart, dpart, tok, resid, gain, gain_lat),
    )


def rms_norm(values, gain_row):
    wide = values.astype(F32)
    scale = lax.rsqrt(jnp.mean(wide * wide, axis=-1, keepdims=True) + NORM_EPSILON)
    return (wide * scale * gain_row).astype(BF)


def split_heads(values):
    return values.reshape(values.shape[0], -1, HD)


def merge_heads(values):
    return values.reshape(values.shape[0], -1)


def mm(eq, left, right):
    return jnp.einsum(eq, left, right, preferred_element_type=F32)


def softmax_of(queries, key_rows):
    scores = mm("qhd,khd->hqk", split_heads(queries), split_heads(key_rows)) * HD ** (-0.5)
    raised = jnp.exp(scores - jnp.max(scores, axis=-1, keepdims=True))
    return raised / jnp.sum(raised, axis=-1, keepdims=True)


def mixed_of(prob, value_rows):
    return merge_heads(mm("hqk,khd->qhd", prob.astype(BF), split_heads(value_rows))).astype(BF)


def attend_back(queries, key_rows, value_rows, prob, upstream):
    grad_prob = mm("qhd,khd->hqk", split_heads(upstream), split_heads(value_rows))
    delta = jnp.sum(grad_prob * prob, axis=-1, keepdims=True)
    score = (prob * (grad_prob - delta) * HD ** (-0.5)).astype(BF)
    return (
        merge_heads(mm("hqk,khd->qhd", score, split_heads(key_rows))),
        merge_heads(mm("hqk,qhd->khd", score, split_heads(queries))),
        merge_heads(mm("hqk,qhd->khd", prob.astype(BF), split_heads(upstream))),
    )


def only_when(flag, compute):
    def skipped():
        return jax.tree.map(lambda x: jnp.zeros(x.shape, x.dtype), jax.eval_shape(compute))

    return lax.cond(flag, compute, skipped)


def shards(section_tokens, w_qkv, w_out, gains, cotangent):
    n, count = dims()
    tok = section_tokens[0, 0]
    cot = cotangent[0]
    rows = tok.shape[0]
    half = rows // 2
    width = HEADS * HD // count
    is_encoder = lax.axis_index("section") == 0
    r = lax.axis_index("render")
    strips = w_qkv[0].reshape(w_qkv.shape[1], 3, count, width)
    qw = lax.dynamic_index_in_dim(strips, r, 2, keepdims=False).reshape(w_qkv.shape[1], 3 * width)
    qfull, ofull, tfull, cfull = gather(qw, w_out[0], tok, cot)

    normed = rms_norm(tfull, gains)
    proj = jnp.dot(normed, qfull, preferred_element_type=F32).astype(BF)
    keys, values = proj[:, width : 2 * width], proj[:, 2 * width :]

    def latent_rows(x):
        return x.reshape(count, rows, -1)[:, half:].reshape(count * half, -1)

    def encoder_forward():
        mixed = mixed_of(softmax_of(latent_rows(proj[:, :width]), keys), values)
        return mixed, jnp.dot(mixed, ofull, preferred_element_type=F32).astype(BF)

    enc_mixed, zpart = only_when(is_encoder, encoder_forward)
    latent, _ = section_hop(0, False, zpart, tok[half:], gains)

    def decoder_attention():
        lat_norm = rms_norm(latent, gains)
        lat_kv = jnp.dot(lat_norm, qfull[:, width:], preferred_element_type=F32).astype(BF)
        lats = lat_kv.shape[0]
        grad_mixed = mm("nd,cd->nc", cfull, ofull).astype(BF)
        mixeds, grads, lat_sum = [], [], 0.0
        for view in range(count):
            at = slice(view * rows, (view + 1) * rows)
            query = proj[at, :width]
            key_rows = jnp.concatenate([lat_kv[:, :width], keys[at]], 0)
            value_rows = jnp.concatenate([lat_kv[:, width:], values[at]], 0)
            prob = softmax_of(query, key_rows)
            mixeds.append(mixed_of(prob, value_rows))
            dq, dk, dv = attend_back(query, key_rows, value_rows, prob, grad_mixed[at])
            lat_sum = lat_sum + jnp.concatenate([dk[:lats], dv[:lats]], 1)
            grads.append(jnp.concatenate([dq, dk[lats:], dv[lats:]], 1).astype(BF))
        lat_grad = lat_sum.astype(BF)
        dnz = mm("nc,dc->nd", lat_grad, qfull[:, width:]).astype(BF)
        return jnp.concatenate(mixeds, 0), jnp.concatenate(grads, 0), lat_norm, lat_grad, dnz

    dec_mixed, dec_grad, lat_norm, lat_grad, dnz = only_when(
        jnp.logical_not(is_encoder), decoder_attention
    )
    dz, gain_lat = section_hop(1, True, dnz, latent, gains)

    def encoder_back():
        query = latent_rows(proj[:, :width])
        prob = softmax_of(query, keys)
        grad_mixed = mm("nd,cd->nc", dz, ofull).astype(BF)
        opart = mm("nc,nd->cd", enc_mixed, dz).astype(BF)
        dq, dk, dv = attend_back(query, keys, values, prob, grad_mixed)
        dq = dq.astype(BF)
        spread = jnp.pad(dq.reshape(count, half, width), ((0, 0), (half, 0), (0, 0)))
        grad = jnp.concatenate(
            [spread.reshape(count * rows, width), dk.astype(BF), dv.astype(BF)], 1
        )
        qpart = mm("nd,nc->dc", normed, grad).astype(BF)
        dn = mm("nc,dc->nd", grad, qfull).astype(BF)
        own = lax.dynamic_slice_in_dim(dz, r * half, half, 0)
        return qpart, opart, dn, jnp.pad(own, ((half, 0), (0, 0)))

    def decoder_back():
        opart = mm("nc,nd->cd", dec_mixed, cfull).astype(BF)
        both = jnp.concatenate([normed, lat_norm], 0)
        lat_all = jnp.pad(lat_grad, ((0, 0), (width, 0)))
        qpart = mm("nd,nc->dc", both, jnp.concatenate([dec_grad, lat_all], 0)).astype(BF)
        dn = mm("nc,dc->nd", dec_grad, qfull).astype(BF)
        return qpart, opart, dn, cot

    qpart, opart, dn, resid = lax.cond(is_encoder, encoder_back, decoder_back)
    qsum, osum, token_grad, gain_grad = reduce_all(qpart, opart, dn, tok, resid, gains, gain_lat)
    qsum = qsum.reshape(count, -1, 3, width).transpose(1, 2, 0, 3).reshape(w_qkv.shape)
    return (
        token_grad[None, None],
        qsum.astype(F32),
        osum.astype(F32)[None],
        gain_grad,
    )


def solution(mesh):
    in_specs = (
        P("section", "dp", "render", None),
        P("section", "dp", None),
        P("section", "dp", None),
        P("section", None),
        P("dp", "render", None),
    )
    out_specs = (
        P("section", "dp", "render", None),
        P("section", "dp", None),
        P("section", "dp", None),
        P("section", None),
    )
    return jax.shard_map(shards, mesh=mesh, in_specs=in_specs, out_specs=out_specs, check_vma=False)
```

time: 729 us -> 343 us (0.47)
  waiting for transfers between devices: 547 us -> 0 us
  Pallas kernels: 0 us -> 266 us
  other arithmetic: 41.6 us -> 1.68 us
  blocking collectives: 34.9 us -> 0 us
  between operations: 14.8 us -> 0.77 us
  matrix products: 40.2 us -> 31.4 us
    reduce_scatter x4 -> x0, waiting for transfers between devices: 293 us -> none  [the longest x1 211 us: shards(): lax.psum_scatter(qkv_part.astype(jnp.bfloat16), 'dp', scatter_dimension=0...]
    pallas_call x0 -> x4, Pallas kernels: none -> 266 us  [call(): pl.pallas_call(body, out_shape=outs, in_specs=in_specs, out_specs=out_spe...]
    all_gather x5 -> x0, waiting for transfers between devices: 196 us -> none  [the longest x1 101 us: shards(): lax.all_gather(qkv_piece, 'dp', axis=0, tiled=True)]
    ppermute x2 -> x0, waiting for transfers between devices: 58.1 us -> none  [shifted(): return lax.ppermute(block, axis, route)]
    psum x1 -> x0, blocking collectives: 32.6 us -> none  [shards(): gain_total = lax.psum(gain_part, ('render', 'dp'))]
    cond x11 -> x0, local copies, waits for them, and re-layouts: 20.3 us -> none  [the longest x3 20.3 us: only_when(): return lax.cond(flag, compute, skipped)]
    concatenate x2 -> x0, other arithmetic: 15.7 us -> none  [the longest x1 14.6 us: encoder_finish(): jnp.concatenate([query_weight_part, key_weight_part], 1)]
    select_n x3 -> x0, other arithmetic: 15.5 us -> none  [the longest x1 10.8 us: shards(): jnp.where(is_encoder, enc_qkv_part, dec_qkv_part).astype(jnp.float32)]
  transfers between devices with their start and end apart: 12 -> 0, of which waited for: 11 -> 0; matrix products, arithmetic and copies ran while one was open for 10% -> 0% of each run, Pallas kernels for 0% -> 0%
where the time goes in v1:
time: 343 us; the launch traced here: 342 us
  Pallas kernels  266 us (78%)
  local copies, waits for them, and re-layouts  41.1 us (12%)
  matrix products  31.4 us (9%)
    pallas_call x4, Pallas kernels, call(): pl.pallas_call(body, out_shape=outs, in_specs=in_specs, out_specs=out_spe...  266 us
    dot_general x10, matrix products, mm(): return jnp.einsum(eq, left, right, preferred_element_type=F32)  24.8 us
    another operation x27, local copies, waits for them, and re-layouts  15.6 us
    unnamed x19, local copies, waits for them, and re-layouts  9.12 us

profile of v1, /device:TPU:0, one launch (start us, length us, event | category | flops | bytes accessed | tf_op | source)
XLA Modules:
  0.0 341.8 jit_solution(194899261970469063)
XLA Ops:
  2.6 1.7 copy.136
  6.8 86.3 %shard_map.84 = (bf16[2048,1536]{1,0:T(8,128)(2,1)S(1)}, bf16[512,2048]{1,0:T(8,128)(2,1)}, bf16[256,2048]{1,0:T(8,128)(2,1)S(1)}, bf16[256,2048]{1,0:T(8,128)(2,1)}) custom-call(bf16[256,1536]{1,0:T(8,128)(2,1)S(1)} %copy.137.qw, bf16[128,2048]{1,0:T(8,128)(2,1)S(1)} %bitcast.213, bf16[128,2048]{1,0:T(8,128)(2,1)S(1)} %bitcast.210, ...), custom_call_target="tpu_custom_call" | custom-call | tf_op jit(solution)/shard_map/pallas_call | solution.py:54
  93.7 2.7 convolution_convert_fusion.13
  96.5 1.9 fusion.157
  98.4 13.0 %conditional.4 = (bf16[128,512]{0,1:T(8,128)(2,1)}, bf16[128,2048]{1,0:T(8,128)(2,1)}) conditional(s32[]{:T(128)} %convert_element_type.166, () %tuple.36, (bf16[256,1536]{1,0:T(8,128)(2,1)}, bf16[256,512]{1,0:T(8,128)(2,1)}, bf16[256,512]{1,0:T(8,128)(2,1)}, bf16[512,2048]{1,0:T(8,128)(2,1)S(1)}) %tuple.80), branch_computations={%region_1.2_spmd, %region_2.5_spmd} | conditional | flops 370344960 | bytes 6557712 | solution.py:522
  98.4 1.8 copy.138
  104.1 2.0 convolution_multiply_fusion
  106.1 3.1 convolution_convert_fusion.1
  109.2 2.2 convolution_convert_fusion
  111.4 9.6 %shard_map.85 = (bf16[128,2048]{1,0:T(8,128)(2,1)}, f32[1,2048]{1,0:T(1,128)}) custom-call(bf16[128,2048]{1,0:T(8,128)(2,1)} %get-tuple-element.122.part, bf16[64,2048]{1,0:T(8,128)(2,1)S(1)} %slice_bitcast_fusion.base, f32[1,2048]{1,0:T(1,128)S(1)} %copy-done.25), custom_call_target="tpu_custom_call" | custom-call | tf_op jit(solution)/shard_map/pallas_call | solution.py:54
  121.0 4.1 %conditional.5 = (bf16[256,512]{0,1:T(8,128)(2,1)}, bf16[256,1536]{0,1:T(8,128)(2,1)}, bf16[128,2048]{1,0:T(8,128)(2,1)}, bf16[128,1024]{0,1:T(8,128)(2,1)}, bf16[128,2048]{1,0:T(8,128)(2,1)}) conditional(s32[]{:T(128)} %convert_element_type.169, () %tuple.35, (bf16[128,2048]{1,0:T(8,128)(2,1)}, f32[1,2048]{1,0:T(1,128)S(1)}, ...), branch_computations={%region_5.6_spmd, %region_6.14_spmd} | conditional | flops 2164267520 | bytes 49051912 | solution.py:522
  125.1 77.6 %shard_map.86 = (bf16[128,2048]{1,0:T(8,128)(2,1)}, f32[1,2048]{1,0:T(1,128)S(1)}) custom-call(bf16[128,2048]{1,0:T(8,128)(2,1)} %get-tuple-element.129.part, bf16[128,2048]{1,0:T(8,128)(2,1)} %get-tuple-element.123.base, f32[1,2048]{1,0:T(1,128)S(1)} %copy-done.25), custom_call_target="tpu_custom_call" | custom-call | tf_op jit(solution)/shard_map/pallas_call | solution.py:54
  202.7 33.0 %conditional.6 = (bf16[512,2048]{1,0:T(8,128)(2,1)S(1)}, bf16[256,2048]{1,0:T(8,128)(2,1)}, bf16[128,2048]{1,0:T(8,128)(2,1)S(1)}, bf16[2048,1536]{1,0:T(8,128)(2,1)}) conditional(s32[]{:T(128)} %convert_element_type.166, (bf16[256,2048]{1,0:T(8,128)(2,1)}, bf16[128,2048]{1,0:T(8,128)(2,1)}, bf16[128,1024]{0,1:T(8,128)(2,1)}, ...), branch_computations={%region_14.15_spmd, %region_15.19_spmd} | conditional | flops 4573233152 | bytes 58859888
  202.9 1.9 convolution_convert_fusion.12
  207.9 2.6 fusion.107
  210.5 2.6 convolution_convert_fusion.9
  215.1 5.7 %fusion.112 = bf16[256,2048]{1,0:T(8,128)(2,1)} fusion(bf16[2048,1536]{1,0:T(8,128)(2,1)} %get-tuple-element.91, bf16[256,512]{0,1:T(8,128)(2,1)S(1)} %bitcast.255, bf16[256,512]{0,1:T(8,128)(2,1)S(1)} %bitcast.253, bf16[256,512]{0,1:T(8,128)(2,1)S(1)} %copy.135), kind=kOutput, calls=%fused_computation.140 | convolution fusion | flops 1612972032 | bytes 8126464 | tf_op jit(solution)/shard_map/cond/branch_1_fun/nc,dc->nd/dot_general | solution.py:494
  220.8 1.7 fusion.160
  222.6 4.4 %fusion.100 = bf16[2048,1536]{0,1:T(8,128)(2,1)} fusion(bf16[256,2048]{1,0:T(8,128)(2,1)S(1)} %copy-done.10, bf16[256,512]{0,1:T(8,128)(2,1)S(1)} %bitcast.256, bf16[256,512]{0,1:T(8,128)(2,1)S(1)} %bitcast.254, bf16[256,512]{0,1:T(8,128)(2,1)S(1)} %copy-done.15), kind=kOutput, calls=%fused_computation.123 | convolution fusion | flops 1616117760 | bytes 8126464 | tf_op jit(solution)/shard_map/cond/branch_1_fun/nd,nc->dc/dot_general | solution.py:494
  227.0 8.6 %copy.164 = bf16[2048,1536]{1,0:T(8,128)(2,1)} copy(bf16[2048,1536]{0,1:T(8,128)(2,1)} %fusion.100) | data formatting | bytes 12582912 | tf_op jit(solution)/shard_map/conditional
  236.9 92.8 %shard_map.87 = (bf16[2,256,1536]{2,1,0:T(8,128)(2,1)S(1)}, bf16[128,2048]{1,0:T(8,128)(2,1)S(1)}, bf16[128,2048]{1,0:T(8,128)(2,1)S(1)}, f32[1,2048]{1,0:T(1,128)S(1)}) custom-call(bf16[2048,1536]{1,0:T(8,128)(2,1)} %get-tuple-element.236.qpart, bf16[512,2048]{1,0:T(8,128)(2,1)} %copy-done.2, bf16[256,2048]{1,0:T(8,128)(2,1)} %get-tuple-element.134.dpart, ...), custom_call_target="tpu_custom_call" | custom-call | tf_op jit(solution)/shard_map/pallas_call | solution.py:54
  330.9 2.1 copy.145
  332.9 3.9 %copy.146 = f32[256,3,2,512]{0,3,2,1:T(8,128)} copy(f32[256,3,2,512]{0,3,1,2:T(8,128)} %bitcast.214) | data formatting | bytes 6291456 | tf_op jit(solution)/shard_map/convert_element_type | solution.py:606
  336.9 3.5 %copy.147 = f32[1,256,3072]{2,1,0:T(8,128)} copy(f32[1,256,3072]{1,2,0:T(8,128)} %bitcast.215) | data formatting | bytes 6291456
  (67 shorter events, 21.9 us)
Async XLA Ops:
  4.4 2.4 copy-start
  4.4 2.4 copy-start.1
  6.8 86.6 %copy-start.25 = (f32[1,2048]{1,0:T(1,128)S(1)}, f32[1,2048]{1,0:T(1,128)}, u32[]{:S(2)}) copy-start(f32[1,2048]{1,0:T(1,128)} %gain.5) | copy-start | bytes 24580
  93.1 3.3 copy-start.28
  93.7 2.8 copy-start.8
  93.7 4.7 %copy-start.3 = (bf16[512,2048]{1,0:T(8,128)(2,1)S(1)}, bf16[512,2048]{1,0:T(8,128)(2,1)}, u32[]{:S(2)}) copy-start(bf16[512,2048]{1,0:T(8,128)(2,1)} %get-tuple-element.121) | copy-start | bytes 6291460
  202.9 3.0 copy-start.7
  204.9 2.6 copy-start.5
  213.1 1.0 copy-start.20
  213.7 0.7 copy-start.22
  214.4 0.7 copy-start.14
  215.1 5.7 %copy-start.11 = (bf16[128,2048]{1,0:T(8,128)(2,1)S(1)}, bf16[128,2048]{1,0:T(8,128)(2,1)}, u32[]{:S(2)}) copy-start(bf16[128,2048]{1,0:T(8,128)(2,1)} %get-tuple-element.86) | copy-start | bytes 1572868 | tf_op jit(solution)/shard_map/conditional
  220.8 1.8 copy-start.10
  220.8 1.8 copy-start.15
  220.8 1.8 copy-start.21
  220.8 1.8 copy-start.23
  235.6 1.3 copy-start.2

commit v2 on v1

v2 whole, which is shorter than its diff:
```python
import functools

import jax
import jax.numpy as jnp
from jax import lax
from jax.experimental import pallas as pl
from jax.experimental.pallas import tpu as pltpu
from jax.sharding import PartitionSpec as P

HEADS = 8
HD = 128
NORM_EPSILON = 1e-06
BF = jnp.bfloat16
F32 = jnp.float32
MESH = pl.DeviceIdType.MESH
VMEM = pl.BlockSpec(memory_space=pltpu.VMEM)
ANY = pl.BlockSpec(memory_space=pl.ANY)


def dims():
    return lax.axis_size("dp"), lax.axis_size("render")


def ring_index(pos, n):
    return jnp.where(pos < n // 2, 2 * pos, 2 * (n - 1 - pos) + 1)


def ring_position(index, n):
    return jnp.where(index % 2 == 0, index // 2, n - 1 - index // 2)


def pieces_of(out_rows):
    return max(1, min(4, out_rows // 32))


def rows_at(start, size):
    return pl.ds(pl.multiple_of(start, 8), size)


def signal(**where):
    pl.semaphore_signal(
        pltpu.get_barrier_semaphore(), inc=1, device_id=where, device_id_type=MESH
    )


def remote(src, dst, send, recv, **where):
    return pltpu.make_async_remote_copy(
        src_ref=src, dst_ref=dst, send_sem=send, recv_sem=recv,
        device_id=where, device_id_type=MESH,
    )


def call(body, collective_id, outs, in_specs, out_specs, scratch, limit, args):
    return pl.pallas_call(
        body,
        out_shape=outs,
        in_specs=in_specs,
        out_specs=out_specs,
        scratch_shapes=scratch,
        compiler_params=pltpu.CompilerParams(
            collective_id=collective_id, has_side_effects=True, vmem_limit_bytes=limit << 20
        ),
    )(*args)


def gather_kernel(n, count, qw, ow, tok, cot, qfull, ofull, tfull, cfull,
                  local, qsend, qrecv, osend, orecv, tsend, trecv):
    me = lax.axis_index("dp")
    r = lax.axis_index("render")
    pos = ring_position(me, n)
    hop = [ring_index((pos + 1) % n, n), ring_index((pos + n - 1) % n, n)]
    per = n // count
    q_rows, o_rows = qw.shape[0], ow.shape[0]
    pieces = pieces_of(o_rows)
    qr, orr = q_rows // (2 * pieces), o_rows // (2 * pieces)
    t_rows = tok.shape[0]
    for where in hop:
        signal(dp=where)
    for j in range(1, count):
        signal(render=(r + j) % count)
    pl.semaphore_wait(pltpu.get_barrier_semaphore(), 1 + count)

    def q_at(ref, shard, d, k):
        return ref.at[rows_at(shard * q_rows + (d * pieces + k) * qr, qr)]

    def o_at(ref, shard, d, k):
        return ref.at[rows_at((shard % per) * o_rows + (d * pieces + k) * orr, orr)]

    own_out = me // per == r
    keep = [
        pltpu.make_async_copy(qw, qfull.at[rows_at(me * q_rows, q_rows)], local.at[0]),
        pltpu.make_async_copy(tok, tfull.at[rows_at(r * t_rows, t_rows)], local.at[2]),
        pltpu.make_async_copy(cot, cfull.at[rows_at(r * t_rows, t_rows)], local.at[3]),
    ]
    keep_out = pltpu.make_async_copy(
        ow, ofull.at[rows_at((me % per) * o_rows, o_rows)], local.at[1]
    )

    def token_copies(j, sender):
        where = rows_at(sender * t_rows, t_rows)
        peer = (r + j) % count
        return [
            remote(tok, tfull.at[where], tsend.at[0, j], trecv.at[0, j], render=peer),
            remote(cot, cfull.at[where], tsend.at[1, j], trecv.at[1, j], render=peer),
        ]

    for j in range(1, count):
        for c in token_copies(j, r):
            c.start()

    for d in range(2):
        for k in range(pieces):
            remote(qw.at[pl.ds((d * pieces + k) * qr, qr)], q_at(qfull, me, d, k),
                   qsend.at[d, 0, k], qrecv.at[d, 0, k], dp=hop[d]).start()

            @pl.when(own_out)
            def _():
                remote(ow.at[pl.ds((d * pieces + k) * orr, orr)], o_at(ofull, me, d, k),
                       osend.at[d, 0, k], orecv.at[d, 0, k], dp=hop[d]).start()

    for c in keep:
        c.start()

    @pl.when(own_out)
    def _():
        keep_out.start()

    def shard_at(d, s):
        return ring_index((pos + n - s) % n if d == 0 else (pos + s) % n, n)

    def q_copy(d, s, k, shard):
        ref = q_at(qfull, shard, d, k)
        return remote(ref, ref, qsend.at[d, s, k], qrecv.at[d, s, k], dp=hop[d])

    def o_copy(d, s, k, shard):
        ref = o_at(ofull, shard, d, k)
        return remote(ref, ref, osend.at[d, s, k], orecv.at[d, s, k], dp=hop[d])

    def step(s, last):
        for k in range(pieces):
            for d in range(2):
                shard = shard_at(d, s)
                q_copy(d, s - 1, k, shard).wait_recv()
                if not last:
                    q_copy(d, s, k, shard).start()

                @pl.when(shard // per == r)
                def _():
                    o_copy(d, s - 1, k, shard).wait_recv()
                    if not last:
                        o_copy(d, s, k, shard).start()

    @pl.loop(1, n - 1)
    def _(s):
        step(s, False)

    step(n - 1, True)

    @pl.loop(0, n - 1)
    def _(s):
        for k in range(pieces):
            for d in range(2):
                shard = shard_at(d, s)
                q_copy(d, s, k, shard).wait_send()

                @pl.when(shard // per == r)
                def _():
                    o_copy(d, s, k, shard).wait_send()

    for c in keep:
        c.wait()

    @pl.when(own_out)
    def _():
        keep_out.wait()

    for j in range(1, count):
        for c in token_copies(j, (r + count - j) % count):
            c.wait_send()
            c.wait_recv()


def gather(qw, ow, tok, cot):
    n, count = dims()
    pieces = pieces_of(ow.shape[0])
    sem = lambda *shape: pltpu.SemaphoreType.DMA(shape)
    shape = lambda rows, like: jax.ShapeDtypeStruct((rows, like.shape[1]), BF)
    ring = (2, n - 1, pieces)
    return call(
        functools.partial(gather_kernel, n, count), 0,
        (shape(n * qw.shape[0], qw), shape(n // count * ow.shape[0], ow),
         shape(count * tok.shape[0], tok), shape(count * cot.shape[0], cot)),
        [ANY] * 4, (ANY,) * 4,
        [sem(4), sem(*ring), sem(*ring), sem(*ring), sem(*ring), sem(2, count), sem(2, count)],
        16, (qw, ow, tok, cot),
    )


def dg(left, right, a, b):
    return lax.dot_general(
        left, right, (((a,), (b,)), ((), ())), preferred_element_type=F32
    )


def softmax(queries, keys):
    scores = dg(queries, keys, 1, 1) * HD ** (-0.5)
    raised = jnp.exp(scores - jnp.max(scores, axis=-1, keepdims=True))
    return raised / jnp.sum(raised, axis=-1, keepdims=True)


def score_grad(prob, upstream, values):
    grad_prob = dg(upstream, values, 1, 1)
    delta = jnp.sum(grad_prob * prob, axis=-1, keepdims=True)
    return (prob * (grad_prob - delta) * HD ** (-0.5)).astype(BF)


def inverse_rms(wide):
    return lax.rsqrt(jnp.mean(wide * wide, axis=-1, keepdims=True) + NORM_EPSILON)


def norm_back(wide, gain_row, grad):
    scale = inverse_rms(wide)
    scaled = grad * gain_row
    inner = jnp.sum(scaled * wide, axis=-1, keepdims=True)
    back = scale * scaled - wide * (scale**3 * inner / wide.shape[-1])
    return back, jnp.sum(grad * wide * scale, axis=0, keepdims=True)


def middle_kernel(count, width, tok, gain, proj, ofull, cfull, qfull,
                  dz, gain_lat, lat_norm, lat_grad, dec_mixed, grads, enc_mixed, enc_prob,
                  zfull, part, own, got, wkv, lat_kv, gmix,
                  wsem, psend, precv, xsend, xrecv, fsend, frecv):
    r = lax.axis_index("render")
    section = lax.axis_index("section")
    rows = proj.shape[0] // count
    half = rows // 2
    lats = count * half
    for j in range(1, count):
        signal(render=(r + j) % count)
    signal(section=1 - section)
    mine = rows_at(r * half, half)
    gain_lat[...] = jnp.zeros_like(gain_lat)
    weights = pltpu.make_async_copy(qfull.at[:, pl.ds(width, 2 * width)], wkv, wsem)

    def partial(j):
        return remote(part.at[rows_at((r + j) % count * half, half)], got.at[j - 1],
                      psend.at[j - 1], precv.at[j - 1], render=(r + j) % count)

    def summed():
        for j in range(1, count):
            partial(j).start()
        total = part[mine].astype(F32)
        for j in range(1, count):
            partial(j).wait_recv()
            total = total + got[j - 1].astype(F32)
        return total

    def across(dst):
        return remote(own, dst.at[mine], xsend, xrecv, section=1 - section)

    def leave(dst):
        across(dst).start()
        across(dst).wait_send()
        for j in range(1, count):
            partial(j).wait_send()

    def arrive(dst):
        across(dst).wait_recv()

        def forward(j, sender):
            ref = dst.at[rows_at(sender * half, half)]
            return remote(ref, ref, fsend.at[j - 1], frecv.at[j - 1], render=(r + j) % count)

        for j in range(1, count):
            forward(j, r).start()
        for j in range(1, count):
            forward(j, r).wait_send()
            forward(j, (r + count - j) % count).wait_recv()

    def head(h, strip):
        return pl.ds(strip * width + h * HD, HD)

    @pl.when(section == 0)
    def _():
        for h in range(width // HD):
            query = jnp.concatenate(
                [proj[pl.ds(v * rows + half, half), head(h, 0)] for v in range(count)], 0
            )
            prob = softmax(query, proj[:, head(h, 1)])
            enc_prob[pl.ds(h * lats, lats)] = prob
            enc_mixed[:, head(h, 0)] = dg(prob.astype(BF), proj[:, head(h, 2)], 1, 0).astype(BF)
        part[...] = dg(enc_mixed[...], ofull[...], 1, 0).astype(BF)
        pl.semaphore_wait(pltpu.get_barrier_semaphore(), count)
        own[...] = (tok[pl.ds(half, half)].astype(F32) + summed()).astype(BF)
        leave(zfull)
        arrive(dz)

    @pl.when(section == 1)
    def _():
        weights.start()
        gmix[...] = dg(cfull[...], ofull[...], 1, 1).astype(BF)
        pl.semaphore_wait(pltpu.get_barrier_semaphore(), count)
        weights.wait()
        arrive(zfull)
        wide = zfull[...].astype(F32)
        lat_norm[...] = (wide * inverse_rms(wide) * gain[...]).astype(BF)
        lat_kv[...] = dg(lat_norm[...], wkv[...], 1, 0).astype(BF)
        for h in range(width // HD):
            lat_key = lat_kv[:, head(h, 0)]
            lat_value = lat_kv[:, head(h, 1)]
            key_sum = jnp.zeros((lats, HD), F32)
            value_sum = jnp.zeros((lats, HD), F32)
            for v in range(count):
                at = pl.ds(v * rows, rows)
                query = proj[at, head(h, 0)]
                keys = jnp.concatenate([lat_key, proj[at, head(h, 1)]], 0)
                values = jnp.concatenate([lat_value, proj[at, head(h, 2)]], 0)
                prob = softmax(query, keys)
                rounded = prob.astype(BF)
                dec_mixed[at, head(h, 0)] = dg(rounded, values, 1, 0).astype(BF)
                upstream = gmix[at, head(h, 0)]
                score = score_grad(prob, upstream, values)
                grads[at, head(h, 0)] = dg(score, keys, 1, 0).astype(BF)
                grad_key = dg(score, query, 0, 0)
                grad_value = dg(rounded, upstream, 0, 0)
                grads[at, head(h, 1)] = grad_key[lats:].astype(BF)
                grads[at, head(h, 2)] = grad_value[lats:].astype(BF)
                key_sum = key_sum + grad_key[:lats]
                value_sum = value_sum + grad_value[:lats]
            lat_grad[:, head(h, 0)] = key_sum.astype(BF)
            lat_grad[:, head(h, 1)] = value_sum.astype(BF)
        part[...] = dg(lat_grad[...], wkv[...], 1, 1).astype(BF)
        grad = summed().astype(BF).astype(F32)
        back, gain_term = norm_back(zfull[mine].astype(F32), gain[...], grad)
        own[...] = back.astype(BF)
        gain_lat[...] = gain_term
        leave(dz)


def middle(tok, gain, proj, ofull, cfull, qfull):
    _, count = dims()
    rows, depth = tok.shape
    half = rows // 2
    lats = count * half
    width = proj.shape[1] // 3
    sem = lambda *shape: pltpu.SemaphoreType.DMA(shape)
    out = lambda *shape, t=BF: jax.ShapeDtypeStruct(shape, t)
    return call(
        functools.partial(middle_kernel, count, width), 1,
        (out(lats, depth), out(1, depth, t=F32), out(lats, depth), out(lats, 2 * width),
         out(count * rows, width), out(count * rows, 3 * width), out(lats, width),
         out(width // HD * lats, count * rows, t=F32)),
        [VMEM] * 5 + [ANY], (VMEM,) * 8,
        [pltpu.VMEM((lats, depth), BF), pltpu.VMEM((lats, depth), BF),
         pltpu.VMEM((half, depth), BF), pltpu.VMEM((count - 1, half, depth), BF),
         pltpu.VMEM((depth, 2 * width), BF), pltpu.VMEM((lats, 2 * width), BF),
         pltpu.VMEM((count * rows, width), BF),
         pltpu.SemaphoreType.DMA, sem(count - 1), sem(count - 1),
         pltpu.SemaphoreType.DMA, pltpu.SemaphoreType.DMA, sem(count - 1), sem(count - 1)],
        40, (tok, gain, proj, ofull, cfull, qfull),
    )


def reduce_kernel(n, count, width, norm_t, proj, enc_prob, enc_mixed, dec_mixed, dec_grads, lat_norm,
                  lat_grad, dz, cfull, ofull, tok, gain, gain_lat, qfull,
                  qout, oout, tout, gout,
                  weights, grads, lat_t, gmix, qpart, opart, dpart,
                  qbuf, obuf, dbuf, gbuf, own_gain, wsem,
                  qsend, qrecv, osend, orecv, dsend, drecv, gsend, grecv, fsend, frecv, hsend, hrecv):
    me = lax.axis_index("dp")
    r = lax.axis_index("render")
    section = lax.axis_index("section")
    pos = ring_position(me, n)
    hop = [ring_index((pos + 1) % n, n), ring_index((pos + n - 1) % n, n)]
    per = n // count
    q_rows, o_rows = norm_t.shape[0] // n, opart.shape[0] // per
    pieces = pieces_of(o_rows)
    qr, orr = q_rows // (2 * pieces), o_rows // (2 * pieces)
    t_rows = tok.shape[0]
    half = t_rows // 2
    lats = count * half
    everyone = n * count
    flat = me * count + r
    load = pltpu.make_async_copy(qfull, weights, wsem)
    load.start()

    @pl.loop(1, everyone)
    def _(j):
        other = (flat + j) % everyone
        signal(dp=other // count, render=other % count)

    @pl.when(section == 0)
    def _():
        opart[...] = dg(enc_mixed[...], dz[...], 0, 0).astype(BF)

    @pl.when(section == 1)
    def _():
        opart[...] = dg(dec_mixed[...], cfull[...], 0, 0).astype(BF)
        lat_t[...] = lat_norm[...].T

    pl.semaphore_wait(pltpu.get_barrier_semaphore(), everyone - 1)

    def o_rows_of(shard, d, k):
        return rows_at((shard % per) * o_rows + (d * pieces + k) * orr, orr)

    def shard_at(d, s):
        return ring_index((pos + 2 * n - 1 - s) % n if d == 0 else (pos + 1 + s) % n, n)

    def q_copy(src, d, s, k):
        return remote(src, qbuf.at[d, s, k], qsend.at[d, s, k], qrecv.at[d, s, k], dp=hop[d])

    def o_copy(src, d, s, k):
        return remote(src, obuf.at[d, s, k], osend.at[d, s, k], orecv.at[d, s, k], dp=hop[d])

    def block(j):
        peer = (r + j) % count
        return remote(dpart.at[rows_at(peer * t_rows, t_rows)], dbuf.at[j - 1],
                      dsend.at[j - 1], drecv.at[j - 1], render=peer)

    def o_step(s):
        for k in range(pieces):
            for d in range(2):
                shard = shard_at(d, s)

                @pl.when(shard // per == r)
                def _():
                    held = obuf.at[d, s - 1, k]
                    o_copy(held, d, s - 1, k).wait_recv()
                    held[...] = (
                        held[...].astype(F32) + opart[o_rows_of(shard, d, k)].astype(F32)
                    ).astype(BF)
                    o_copy(held, d, s, k).start()

    for k in range(pieces):
        for d in range(2):
            shard = shard_at(d, 0)

            @pl.when(shard // per == r)
            def _():
                o_copy(opart.at[o_rows_of(shard, d, k)], d, 0, k).start()

    def head(h, strip):
        return pl.ds(strip * width + h * HD, HD)

    @pl.when(section == 0)
    def _():
        gmix[...] = dg(dz[...], ofull[...], 1, 1).astype(BF)
        for v in range(count):
            grads[pl.ds(v * t_rows, half), pl.ds(0, width)] = jnp.zeros((half, width), BF)

    @pl.when(section == 1)
    def _():
        grads[...] = dec_grads[...]

    for h in range(width // HD):
        @pl.when(section == 0)
        def _():
            prob = enc_prob[pl.ds(h * lats, lats)]
            upstream = gmix[:, head(h, 0)]
            query = jnp.concatenate(
                [proj[pl.ds(v * t_rows + half, half), head(h, 0)] for v in range(count)], 0
            )
            score = score_grad(prob, upstream, proj[:, head(h, 2)])
            grad_query = dg(score, proj[:, head(h, 1)], 1, 0).astype(BF)
            for v in range(count):
                grads[pl.ds(v * t_rows + half, half), head(h, 0)] = (
                    grad_query[v * half : (v + 1) * half]
                )
            grads[:, head(h, 1)] = dg(score, query, 0, 0).astype(BF)
            grads[:, head(h, 2)] = dg(prob.astype(BF), upstream, 0, 0).astype(BF)

        if h < n - 2:
            o_step(h + 1)

    def own_part(shard, d):
        at = rows_at(shard * q_rows + d * pieces * qr, pieces * qr)
        term = dg(norm_t[at], grads[...], 1, 0)

        @pl.when(section == 0)
        def _():
            qpart[d] = term.astype(BF)

        @pl.when(section == 1)
        def _():
            lat = dg(lat_t[at], lat_grad[...], 1, 0)
            qpart[d] = jnp.concatenate(
                [term[:, :width], term[:, width:] + lat], 1
            ).astype(BF)

    for d in range(2):
        own_part(shard_at(d, 0), d)
        for k in range(pieces):
            q_copy(qpart.at[d, pl.ds(k * qr, qr)], d, 0, k).start()

    load.wait()
    dpart[...] = dg(grads[...], weights[...], 1, 1).astype(BF)
    for j in range(1, count):
        block(j).start()
    total = dpart[rows_at(r * t_rows, t_rows)].astype(F32)
    for j in range(1, count):
        block(j).wait_recv()
        total = total + dbuf[j - 1].astype(F32)
    back, gain_term = norm_back(tok[...].astype(F32), gain[...], total.astype(BF).astype(F32))
    own_gain[...] = gain_lat[...] + gain_term

    @pl.when(section == 0)
    def _():
        tout[pl.ds(0, half)] = back[:half].astype(BF)
        tout[pl.ds(half, half)] = (back[half:] + dz[rows_at(r * half, half)].astype(F32)).astype(BF)

    @pl.when(section == 1)
    def _():
        tout[...] = (back + cfull[rows_at(r * t_rows, t_rows)].astype(F32)).astype(BF)

    def gain_copy(j, sender):
        other = (flat + j) % everyone
        return remote(own_gain, gbuf.at[sender], gsend.at[j], grecv.at[j],
                      dp=other // count, render=other % count)

    @pl.loop(1, everyone)
    def _(j):
        gain_copy(j, flat).start()

    for d in range(2):
        for k in range(pieces):
            q_copy(qpart.at[d, pl.ds(k * qr, qr)], d, 0, k).wait_send()

    def q_step(s):
        for d in range(2):
            own_part(shard_at(d, s), d)
        for k in range(pieces):
            for d in range(2):
                held = qbuf.at[d, s - 1, k]
                q_copy(held, d, s - 1, k).wait_recv()
                held[...] = (
                    held[...].astype(F32) + qpart[d, pl.ds(k * qr, qr)].astype(F32)
                ).astype(BF)
                q_copy(held, d, s, k).start()

    early = min(width // HD, n - 2)

    @pl.loop(1, n - 1)
    def _(s):
        q_step(s)

        @pl.when(s > early)
        def _():
            o_step(s)

    own_out = me // per == r

    def q_final(j, d, k, sender):
        ref = qout.at[sender, pl.ds((d * pieces + k) * qr, qr)]
        return remote(ref, ref, fsend.at[j - 1, d, k], frecv.at[j - 1, d, k],
                      render=(r + j) % count)

    def o_final(j, d, k):
        ref = oout.at[pl.ds((d * pieces + k) * orr, orr)]
        return remote(ref, ref, hsend.at[j - 1, d, k], hrecv.at[d, k], render=(r + j) % count)

    for d in range(2):
        own_part(me, d)

    for k in range(pieces):
        for d in range(2):
            @pl.when(own_out)
            def _():
                held_out = obuf.at[d, n - 2, k]
                o_copy(held_out, d, n - 2, k).wait_recv()
                oout[pl.ds((d * pieces + k) * orr, orr)] = (
                    held_out[...].astype(F32) + opart[o_rows_of(me, d, k)].astype(F32)
                ).astype(BF)
                for j in range(1, count):
                    o_final(j, d, k).start()

    gbuf[flat] = own_gain[...]

    @pl.loop(1, everyone)
    def _(j):
        gain_copy(j, (flat + everyone - j) % everyone).wait_recv()
        gain_copy(j, flat).wait_send()

    gout[...] = jnp.sum(gbuf[...], axis=0)

    for k in range(pieces):
        for d in range(2):
            held = qbuf.at[d, n - 2, k]
            q_copy(held, d, n - 2, k).wait_recv()
            qout[r, pl.ds((d * pieces + k) * qr, qr)] = (
                held[...].astype(F32) + qpart[d, pl.ds(k * qr, qr)].astype(F32)
            ).astype(BF)
            for j in range(1, count):
                q_final(j, d, k, r).start()

    @pl.loop(0, n - 1)
    def _(s):
        for k in range(pieces):
            for d in range(2):
                shard = shard_at(d, s)

                @pl.when(s > 0)
                def _():
                    q_copy(qbuf.at[d, s, k], d, s, k).wait_send()

                @pl.when(shard // per == r)
                def _():
                    o_copy(obuf.at[d, s, k], d, s, k).wait_send()

    for j in range(1, count):
        block(j).wait_send()
        for k in range(pieces):
            for d in range(2):
                q_final(j, d, k, r).wait_send()
                q_final(j, d, k, (r + count - j) % count).wait_recv()

                @pl.when(own_out)
                def _():
                    o_final(j, d, k).wait_send()

    @pl.when(jnp.logical_not(own_out))
    def _():
        for k in range(pieces):
            for d in range(2):
                o_final(1, d, k).wait_recv()


def reduce_all(*args):
    norm_t, proj, tok, gain = args[0], args[1], args[11], args[12]
    n, count = dims()
    depth = norm_t.shape[0]
    width = proj.shape[1] // 3
    q_rows = depth // n
    o_rows = width * count // n
    pieces = pieces_of(o_rows)
    qr, orr = q_rows // (2 * pieces), o_rows // (2 * pieces)
    lats = tok.shape[0] // 2 * count
    sem = lambda *shape: pltpu.SemaphoreType.DMA(shape)
    ring = (2, n - 1, pieces)
    return call(
        functools.partial(reduce_kernel, n, count, width), 3,
        (jax.ShapeDtypeStruct((count, q_rows, 3 * width), BF),
         jax.ShapeDtypeStruct((o_rows, depth), BF),
         jax.ShapeDtypeStruct(tok.shape, BF),
         jax.ShapeDtypeStruct(gain.shape, F32)),
        [VMEM] * 14 + [ANY], (VMEM,) * 4,
        [pltpu.VMEM((depth, 3 * width), BF), pltpu.VMEM(proj.shape, BF),
         pltpu.VMEM((depth, lats), BF), pltpu.VMEM((lats, width), BF),
         pltpu.VMEM((2, q_rows // 2, 3 * width), BF), pltpu.VMEM((width, depth), BF),
         pltpu.VMEM((proj.shape[0], depth), BF),
         pltpu.VMEM(ring + (qr, 3 * width), BF),
         pltpu.VMEM(ring + (orr, depth), BF),
         pltpu.VMEM((count - 1,) + tok.shape, BF),
         pltpu.VMEM((n * count,) + gain.shape, F32),
         pltpu.VMEM(gain.shape, F32), pltpu.SemaphoreType.DMA,
         sem(*ring), sem(*ring), sem(*ring), sem(*ring),
         sem(count - 1), sem(count - 1), sem(n * count), sem(n * count),
         sem(count - 1, 2, pieces), sem(count - 1, 2, pieces),
         sem(count - 1, 2, pieces), sem(2, pieces)],
        56, args,
    )


def widen_kernel(q_ref, o_ref, qout, oout):
    count, _, wide = q_ref.shape
    width = wide // 3
    for c in range(count):
        for strip in range(3):
            qout[0, :, pl.ds((strip * count + c) * width, width)] = (
                q_ref[c, :, pl.ds(strip * width, width)].astype(F32)
            )
    oout[0] = o_ref[...].astype(F32)


def widen(qsum, osum):
    count, q_rows, wide = qsum.shape
    o_rows, depth = osum.shape
    steps = 4
    qb, ob = q_rows // steps, o_rows // steps
    return pl.pallas_call(
        widen_kernel,
        grid=(steps,),
        out_shape=(jax.ShapeDtypeStruct((1, q_rows, count * wide), F32),
                   jax.ShapeDtypeStruct((1, o_rows, depth), F32)),
        in_specs=[pl.BlockSpec((count, qb, wide), lambda i: (0, i, 0)),
                  pl.BlockSpec((ob, depth), lambda i: (i, 0))],
        out_specs=(pl.BlockSpec((1, qb, count * wide), lambda i: (0, i, 0)),
                   pl.BlockSpec((1, ob, depth), lambda i: (0, i, 0))),
    )(qsum, osum)


def rms_norm(values, gain_row):
    wide = values.astype(F32)
    return (wide * inverse_rms(wide) * gain_row).astype(BF)


def shards(section_tokens, w_qkv, w_out, gains, cotangent):
    n, count = dims()
    tok = section_tokens[0, 0]
    cot = cotangent[0]
    width = HEADS * HD // count
    r = lax.axis_index("render")
    qw = jnp.concatenate(
        [lax.dynamic_slice_in_dim(w_qkv[0], (strip * count + r) * width, width, 1)
         for strip in range(3)], 1
    )
    qfull, ofull, tfull, cfull = gather(qw, w_out[0], tok, cot)
    normed = rms_norm(tfull, gains)
    proj = jnp.dot(normed, qfull, preferred_element_type=F32).astype(BF)
    dz, gain_lat, lat_norm, lat_grad, dec_mixed, dec_grads, enc_mixed, enc_prob = middle(
        tok, gains, proj, ofull, cfull, qfull
    )
    qsum, osum, token_grad, gain_grad = reduce_all(
        normed.T, proj, enc_prob, enc_mixed, dec_mixed, dec_grads, lat_norm, lat_grad,
        dz, cfull, ofull, tok, gains, gain_lat, qfull
    )
    qkv_grad, out_grad = widen(qsum, osum)
    return token_grad[None, None], qkv_grad, out_grad, gain_grad


def solution(mesh):
    in_specs = (
        P("section", "dp", "render", None),
        P("section", "dp", None),
        P("section", "dp", None),
        P("section", None),
        P("dp", "render", None),
    )
    out_specs = (
        P("section", "dp", "render", None),
        P("section", "dp", None),
        P("section", "dp", None),
        P("section", None),
    )
    return jax.shard_map(shards, mesh=mesh, in_specs=in_specs, out_specs=out_specs, check_vma=False)
```

time: 343 us -> 243 us (0.71)
  Pallas kernels: 266 us -> 219 us
  matrix products: 31.4 us -> 5.16 us
  local copies, waits for them, and re-layouts: 41.1 us -> 15.1 us
    pallas_call x4 -> x3, Pallas kernels: 266 us -> 215 us  [call(): pl.pallas_call(body, out_shape=outs, in_specs=in_specs, out_specs=out_spe...]
    dot_general x11 -> x0, matrix products: 27 us -> none  [the longest x10 24.8 us: mm(): return jnp.einsum(eq, left, right, preferred_element_type=F32)]
    another operation x27 -> x0, local copies, waits for them, and re-layouts: 15.6 us -> none
    convert_element_type x4 -> x0, local copies, waits for them, and re-layouts: 6.16 us -> none  [the longest x2 5.99 us: shards(): qsum.astype(F32)]
    slice x6 -> x0, local copies, waits for them, and re-layouts: 5.47 us -> none  [the longest x1 1.89 us: shards(): keys, values = (proj[:, width:2 * width], proj[:, 2 * width:])]
    pallas_call x0 -> x1, Pallas kernels: none -> 4.18 us  [widen(): pl.pallas_call(widen_kernel, grid=(steps,), out_shape=(jax.ShapeDtypeStru...]
    unnamed x19 -> x46, local copies, waits for them, and re-layouts: 9.12 us -> 12.5 us
where the time goes in v2:
time: 243 us
  Pallas kernels  219 us (90%)
  local copies, waits for them, and re-layouts  15.1 us (6%)
  matrix products  5.16 us (2%)
  other arithmetic  3.05 us (1%)
    pallas_call x3, Pallas kernels, call(): pl.pallas_call(body, out_shape=outs, in_specs=in_specs, out_specs=out_spe...  215 us
    unnamed x46, local copies, waits for them, and re-layouts  12.5 us
    dot_general x1, matrix products, shards(): proj = jnp.dot(normed, qfull, preferred_element_type=F32).astype(BF)  5.16 us

profile of v2, /device:TPU:0, one launch (start us, length us, event | category | flops | bytes accessed | tf_op | source)
XLA Modules:
  0.0 243.1 jit_solution(11047126500357390996)
XLA Ops:
  0.7 1.3 dynamic-slice_bitcast_fusion.2
  2.0 0.1 pad_maximum_fusion.qw
  2.1 0.2 copy-done.11
  2.2 86.1 %shard_map.84 = (bf16[2048,1536]{1,0:T(8,128)(2,1)S(1)}, bf16[512,2048]{1,0:T(8,128)(2,1)S(1)}, bf16[256,2048]{1,0:T(8,128)(2,1)S(1)}, bf16[256,2048]{1,0:T(8,128)(2,1)S(1)}) custom-call(bf16[256,1536]{1,0:T(8,128)(2,1)S(1)} %pad_maximum_fusion.qw, bf16[128,2048]{1,0:T(8,128)(2,1)S(1)} %bitcast.19, bf16[128,2048]{1,0:T(8,128)(2,1)S(1)} %bitcast.17, ...), custom_call_target="tpu_custom_call" | custom-call | tf_op jit(solution)/shard_map/pallas_call | solution.py:54
  88.4 2.6 %copy-done = bf16[2048,1536]{1,0:T(8,128)(2,1)} copy-done((bf16[2048,1536]{1,0:T(8,128)(2,1)}, bf16[2048,1536]{1,0:T(8,128)(2,1)S(1)}, u32[]{:S(2)}) %copy-start) | copy-done | bytes 6291480
  91.0 1.3 copy-done.1
  92.4 1.3 copy.9
  93.7 1.7 fusion
  95.4 5.2 %convolution_convert_fusion.proj = bf16[256,1536]{1,0:T(8,128)(2,1)S(1)} fusion(bf16[2048,1536]{1,0:T(8,128)(2,1)} %copy-done, bf16[256,2048]{0,1:T(8,128)(2,1)} %copy.9, f32[2048]{0:T(1024)S(1)} %bitcast.21, f32[256]{0:T(256)S(1)} %add_rsqrt_fusion), kind=kOutput, calls=%fused_computation.2 | convolution fusion | flops 1613103104 | bytes 8135680 | tf_op jit(solution)/shard_map/dot_general | solution.py:708
  100.6 1.3 fusion.4.norm_t
  101.9 0.9 copy-done.2
  102.8 28.2 %shard_map.85 = (bf16[128,2048]{1,0:T(8,128)(2,1)S(1)}, f32[1,2048]{1,0:T(1,128)S(1)}, bf16[128,2048]{1,0:T(8,128)(2,1)S(1)}, bf16[128,1024]{1,0:T(8,128)(2,1)S(...) custom-call(bf16[128,2048]{1,0:T(8,128)(2,1)S(1)} %bitcast.18, ...), custom_call_target="tpu_custom_call" | custom-call | tf_op jit(solution)/shard_map/pallas_call | solution.py:54
  131.1 0.9 copy-done.6
  132.0 0.8 copy-done.7
  132.8 0.8 copy-done.8
  133.6 0.8 copy-done.9
  134.4 0.7 copy-done.12
  135.2 0.7 copy-done.13
  135.9 0.6 copy-done.14
  136.5 0.6 copy-done.16
  137.1 100.3 %shard_map.86 = (bf16[2,256,1536]{2,1,0:T(8,128)(2,1)}, bf16[128,2048]{1,0:T(8,128)(2,1)}, bf16[128,2048]{1,0:T(8,128)(2,1)}, f32[1,2048]{1,0:T(1,128)}) custom-call(bf16[2048,256]{1,0:T(8,128)(2,1)} %fusion.4.norm_t, bf16[256,1536]{1,0:T(8,128)(2,1)} %copy-done.5, f32[512,256]{1,0:T(8,128)} %copy-done.9, bf16[128,512]{1,0:T(8,128)(2,1)} %copy-done.14, ...), custom_call_target="tpu_custom_call" | custom-call | tf_op jit(solution)/shard_map/pallas_call | solution.py:54
  237.5 4.2 %shard_map.87 = (f32[1,256,3072]{2,1,0:T(8,128)}, f32[1,128,2048]{2,1,0:T(8,128)}) custom-call(bf16[2,256,1536]{2,1,0:T(8,128)(2,1)} %get-tuple-element.35.q_ref, bf16[128,2048]{1,0:T(8,128)(2,1)} %get-tuple-element.36.o_ref), custom_call_target="tpu_custom_call" | custom-call | tf_op jit(solution)/shard_map/pallas_call | solution.py:679
  241.7 0.8 copy.12
  242.5 0.6 copy.13
  (34 shorter events, 0.1 us)
Async XLA Ops:
  0.6 1.4 copy-start.3
  0.7 1.4 copy-start.10
  0.7 1.6 copy-start.11
  88.4 2.7 %copy-start = (bf16[2048,1536]{1,0:T(8,128)(2,1)}, bf16[2048,1536]{1,0:T(8,128)(2,1)S(1)}, u32[]{:S(2)}) copy-start(bf16[2048,1536]{1,0:T(8,128)(2,1)S(1)} %get-tuple-element.23.qfull) | copy-start | bytes 18874372
  91.0 1.3 copy-start.1
  92.3 9.6 %copy-start.4 = (bf16[256,2048]{1,0:T(8,128)(2,1)}, bf16[256,2048]{1,0:T(8,128)(2,1)S(1)}, u32[]{:S(2)}) copy-start(bf16[256,2048]{1,0:T(8,128)(2,1)S(1)} %get-tuple-element.25.cfull) | copy-start | bytes 3145732
  92.4 3.0 %copy-start.15 = (f32[1,2048]{1,0:T(1,128)S(1)}, f32[1,2048]{1,0:T(1,128)}, u32[]{:S(2)}) copy-start(f32[1,2048]{1,0:T(1,128)} %gain.3) | copy-start | bytes 24580
  93.7 8.2 %slice-start = ((s8[6291456]{0:T(1024)(128)(4,1)}), s8[4194304]{0:T(1024)(128)(4,1)S(1)}, s32[]{:S(2)}) async-start(s8[6291456]{0:T(1024)(128)(4,1)} %bitcast.14), calls=%async_computation | async-start | bytes 8388608
  95.4 5.2 %copy-start.17 = (bf16[256,2048]{0,1:T(8,128)(2,1)S(1)}, bf16[256,2048]{0,1:T(8,128)(2,1)}, u32[]{:S(2)}) copy-start(bf16[256,2048]{0,1:T(8,128)(2,1)} %copy.9) | copy-start | bytes 3145732
  95.4 6.5 %slice-start.1 = ((s8[6291456]{0:T(1024)(128)(4,1)}), s8[2097152]{0:T(1024)(128)(4,1)S(1)}, s32[]{:S(2)}) async-start(s8[6291456]{0:T(1024)(128)(4,1)} %bitcast.14), calls=%async_computation.1 | async-start | bytes 4194304
  100.6 30.5 %copy-start.5 = (bf16[256,1536]{1,0:T(8,128)(2,1)}, bf16[256,1536]{1,0:T(8,128)(2,1)S(1)}, u32[]{:S(2)}) copy-start(bf16[256,1536]{1,0:T(8,128)(2,1)S(1)} %convolution_convert_fusion.proj) | copy-start | bytes 2359300
  100.6 2.3 copy-start.2
  131.1 0.9 copy-start.6
  132.0 0.8 copy-start.7
  132.8 0.8 copy-start.8
  133.6 0.8 copy-start.9
  134.4 0.7 copy-start.12
  135.2 0.7 copy-start.13
  135.9 0.7 copy-start.14
  136.5 0.6 copy-start.16
  237.5 4.2 %copy-start.18 = (bf16[128,2048]{1,0:T(8,128)(2,1)S(1)}, bf16[128,2048]{1,0:T(8,128)(2,1)}, u32[]{:S(2)}) copy-start(bf16[128,2048]{1,0:T(8,128)(2,1)} %get-tuple-element.34) | copy-start | bytes 1572868
  237.5 5.0 %copy-start.19 = (f32[1,2048]{1,0:T(1,128)S(1)}, f32[1,2048]{1,0:T(1,128)}, u32[]{:S(2)}) copy-start(f32[1,2048]{1,0:T(1,128)} %get-tuple-element.50) | copy-start | bytes 24580

commit v3 on v2

v3 whole, which is shorter than its diff:
```python
import functools

import jax
import jax.numpy as jnp
from jax import lax
from jax.experimental import pallas as pl
from jax.experimental.pallas import tpu as pltpu
from jax.sharding import PartitionSpec as P

HEADS = 8
HD = 128
NORM_EPSILON = 1e-06
BF = jnp.bfloat16
F32 = jnp.float32
MESH = pl.DeviceIdType.MESH
VMEM = pl.BlockSpec(memory_space=pltpu.VMEM)
ANY = pl.BlockSpec(memory_space=pl.ANY)


def dims():
    return lax.axis_size("dp"), lax.axis_size("render")


def ring_index(pos, n):
    return jnp.where(pos < n // 2, 2 * pos, 2 * (n - 1 - pos) + 1)


def ring_position(index, n):
    return jnp.where(index % 2 == 0, index // 2, n - 1 - index // 2)


def pieces_of(out_rows):
    return max(1, min(4, out_rows // 32))


def rows_at(start, size):
    return pl.ds(pl.multiple_of(start, 8), size)


def signal(**where):
    pl.semaphore_signal(
        pltpu.get_barrier_semaphore(), inc=1, device_id=where, device_id_type=MESH
    )


def remote(src, dst, send, recv, **where):
    return pltpu.make_async_remote_copy(
        src_ref=src, dst_ref=dst, send_sem=send, recv_sem=recv,
        device_id=where, device_id_type=MESH,
    )


def call(body, collective_id, outs, in_specs, out_specs, scratch, limit, args):
    return pl.pallas_call(
        body,
        out_shape=outs,
        in_specs=in_specs,
        out_specs=out_specs,
        scratch_shapes=scratch,
        compiler_params=pltpu.CompilerParams(
            collective_id=collective_id, has_side_effects=True, vmem_limit_bytes=limit << 20
        ),
    )(*args)


def dg(left, right, a, b):
    return lax.dot_general(
        left, right, (((a,), (b,)), ((), ())), preferred_element_type=F32
    )


def softmax(queries, keys):
    scores = dg(queries, keys, 1, 1) * HD ** (-0.5)
    raised = jnp.exp(scores - jnp.max(scores, axis=-1, keepdims=True))
    return raised / jnp.sum(raised, axis=-1, keepdims=True)


def score_grad(prob, upstream, values):
    grad_prob = dg(upstream, values, 1, 1)
    delta = jnp.sum(grad_prob * prob, axis=-1, keepdims=True)
    return (prob * (grad_prob - delta) * HD ** (-0.5)).astype(BF)


def inverse_rms(wide):
    return lax.rsqrt(jnp.mean(wide * wide, axis=-1, keepdims=True) + NORM_EPSILON)


def norm_back(wide, gain_row, grad):
    scale = inverse_rms(wide)
    scaled = grad * gain_row
    inner = jnp.sum(scaled * wide, axis=-1, keepdims=True)
    back = scale * scaled - wide * (scale**3 * inner / wide.shape[-1])
    return back, jnp.sum(grad * wide * scale, axis=0, keepdims=True)


def step_kernel(n, count, width, qw, ow, tok, cot, gain,
                qout, oout, tout, gout,
                qfull, ofull, tfull, cfull, norm_t, acc, proj, enc_prob, mixed, gmix,
                lat_norm, lat_t, lat_kv, lat_grad, grads, zfull, dz, part, own, got, gain_lat,
                qpart, opart, dpart, qbuf, obuf, dbuf, gbuf, own_gain,
                gqs, gqr, gos, gor, tsend, trecv, psend, precv, xsend, xrecv, fsend, frecv,
                qsend, qrecv, osend, orecv, dsend, drecv, gsend, grecv, esend, erecv, hsend, hrecv):
    me = lax.axis_index("dp")
    r = lax.axis_index("render")
    section = lax.axis_index("section")
    pos = ring_position(me, n)
    hop = [ring_index((pos + 1) % n, n), ring_index((pos + n - 1) % n, n)]
    per = n // count
    q_rows, o_rows = qw.shape[0], ow.shape[0]
    pieces = pieces_of(o_rows)
    qr, orr = q_rows // (2 * pieces), o_rows // (2 * pieces)
    side = q_rows // 2
    rows = tok.shape[0]
    half = rows // 2
    lats = count * half
    heads = width // HD
    wide_head = 3 * HD
    everyone = n * count
    flat = me * count + r
    own_out = me // per == r
    mine = rows_at(r * half, half)
    barrier = pltpu.get_barrier_semaphore()

    @pl.loop(1, everyone)
    def _(j):
        other = (flat + j) % everyone
        signal(dp=other // count, render=other % count)

    signal(section=1 - section)
    pl.semaphore_wait(barrier, everyone)

    def head(h, strip):
        return pl.ds(h * wide_head + strip * HD, HD)

    def pair(h):
        return pl.ds(h * wide_head + HD, 2 * HD)


    def q_at(shard, d, k):
        return qfull.at[rows_at(shard * q_rows + (d * pieces + k) * qr, qr)]

    def o_rows_of(shard, d, k):
        return rows_at((shard % per) * o_rows + (d * pieces + k) * orr, orr)

    def token_copies(j, sender):
        where = rows_at(sender * rows, rows)
        peer = (r + j) % count
        return [
            remote(tok, tfull.at[where], tsend.at[0, j - 1], trecv.at[0, j - 1], render=peer),
            remote(cot, cfull.at[where], tsend.at[1, j - 1], trecv.at[1, j - 1], render=peer),
        ]

    for j in range(1, count):
        for c in token_copies(j, r):
            c.start()

    def first_q(d, k):
        return remote(qw.at[pl.ds((d * pieces + k) * qr, qr)], q_at(me, d, k),
                      gqs.at[d, 0, k], gqr.at[d, 0, k], dp=hop[d])

    def first_o(d, k):
        return remote(ow.at[pl.ds((d * pieces + k) * orr, orr)], ofull.at[o_rows_of(me, d, k)],
                      gos.at[d, 0, k], gor.at[d, 0, k], dp=hop[d])

    for k in range(pieces):
        for d in range(2):
            first_q(d, k).start()

    for k in range(pieces):
        for d in range(2):
            @pl.when(own_out)
            def _():
                first_o(d, k).start()

    def origin(d, s):
        return ring_index((pos + n - s) % n if d == 0 else (pos + s) % n, n)

    def q_in(d, s, k):
        ref = q_at(origin(d, s), d, k)
        return remote(ref, ref, gqs.at[d, s - 1, k], gqr.at[d, s - 1, k], dp=hop[d])

    def q_on(d, s, k):
        ref = q_at(origin(d, s), d, k)
        return remote(ref, ref, gqs.at[d, s, k], gqr.at[d, s, k], dp=hop[d])

    def o_in(d, s, k):
        ref = ofull.at[o_rows_of(origin(d, s), d, k)]
        return remote(ref, ref, gos.at[d, s - 1, k], gor.at[d, s - 1, k], dp=hop[d])

    def o_on(d, s, k):
        ref = ofull.at[o_rows_of(origin(d, s), d, k)]
        return remote(ref, ref, gos.at[d, s, k], gor.at[d, s, k], dp=hop[d])

    def q_forward(s, last):
        for k in range(pieces):
            for d in range(2):
                q_in(d, s, k).wait_recv()
                if not last:
                    q_on(d, s, k).start()

    def o_forward(s, last):
        for k in range(pieces):
            for d in range(2):
                @pl.when(origin(d, s) // per == r)
                def _():
                    o_in(d, s, k).wait_recv()
                    if not last:
                        o_on(d, s, k).start()

    def project(s):
        for d in range(2):
            at = rows_at(origin(d, s) * q_rows + d * side, side)
            acc[...] += dg(norm_t[at], qfull[at], 0, 0)

    qfull[rows_at(me * q_rows, q_rows)] = qw[...]

    @pl.when(own_out)
    def _():
        ofull[rows_at((me % per) * o_rows, o_rows)] = ow[...]

    tfull[rows_at(r * rows, rows)] = tok[...]
    cfull[rows_at(r * rows, rows)] = cot[...]
    for j in range(1, count):
        for c in token_copies(j, (r + count - j) % count):
            c.wait_recv()
    for v in range(count):
        wide = tfull[pl.ds(v * rows, rows)].astype(F32)
        norm_t[:, pl.ds(v * rows, rows)] = (
            (wide * inverse_rms(wide) * gain[...]).astype(BF).T
        )
    acc[...] = jnp.zeros_like(acc)
    project(0)
    lag = min(2, n - 2)

    @pl.loop(1, n - 1)
    def _(s):
        q_forward(s, False)

        @pl.when(s > lag)
        def _():
            o_forward(s - lag, False)

        project(s)

    q_forward(n - 1, True)
    late = list(range(n - 1 - lag, n))
    o_forward(late[0], late[0] == n - 1)
    project(n - 1)
    proj[...] = acc[...].astype(BF)
    late = late[1:]

    for h in range(heads):
        @pl.when(section == 0)
        def _():
            query = jnp.concatenate(
                [proj[pl.ds(v * rows + half, half), head(h, 0)] for v in range(count)], 0
            )
            prob = softmax(query, proj[:, head(h, 1)])
            enc_prob[pl.ds(h * lats, lats)] = prob
            mixed[pl.ds(0, lats), pl.ds(h * HD, HD)] = dg(
                prob.astype(BF), proj[:, head(h, 2)], 1, 0
            ).astype(BF)

        if late:
            s = late.pop(0)
            o_forward(s, s == n - 1)
    for s in late:
        o_forward(s, s == n - 1)


    def partial(j):
        return remote(part.at[rows_at((r + j) % count * half, half)], got.at[j - 1],
                      psend.at[j - 1], precv.at[j - 1], render=(r + j) % count)

    def summed():
        for j in range(1, count):
            partial(j).start()
        total = part[mine].astype(F32)
        for j in range(1, count):
            partial(j).wait_recv()
            total = total + got[j - 1].astype(F32)
        return total

    def across(dst):
        return remote(own, dst.at[mine], xsend, xrecv, section=1 - section)

    def arrive(dst):
        across(dst).wait_recv()

        def forward(j, sender):
            ref = dst.at[rows_at(sender * half, half)]
            return remote(ref, ref, fsend.at[j - 1], frecv.at[j - 1], render=(r + j) % count)

        for j in range(1, count):
            forward(j, r).start()
        for j in range(1, count):
            forward(j, r).wait_send()
            forward(j, (r + count - j) % count).wait_recv()

    @pl.when(section == 0)
    def _():
        gain_lat[...] = jnp.zeros_like(gain_lat)
        part[...] = dg(mixed[pl.ds(0, lats)], ofull[...], 1, 0).astype(BF)
        own[...] = (tok[pl.ds(half, half)].astype(F32) + summed()).astype(BF)
        across(zfull).start()
        arrive(dz)
        opart[...] = dg(mixed[pl.ds(0, lats)], dz[...], 0, 0).astype(BF)

    @pl.when(section == 1)
    def _():
        gmix[...] = dg(cfull[...], ofull[...], 1, 1).astype(BF)
        arrive(zfull)
        wide = zfull[...].astype(F32)
        lat_norm[...] = (wide * inverse_rms(wide) * gain[...]).astype(BF)
        for h in range(heads):
            both = pl.ds(h * 2 * HD, 2 * HD)
            lat_kv[:, both] = dg(lat_norm[...], qfull[:, pair(h)], 1, 0).astype(BF)
        total = None
        for h in range(heads):
            lat_key = lat_kv[:, pl.ds(h * 2 * HD, HD)]
            lat_value = lat_kv[:, pl.ds(h * 2 * HD + HD, HD)]
            key_sum = jnp.zeros((lats, HD), F32)
            value_sum = jnp.zeros((lats, HD), F32)
            for v in range(count):
                at = pl.ds(v * rows, rows)
                query = proj[at, head(h, 0)]
                keys = jnp.concatenate([lat_key, proj[at, head(h, 1)]], 0)
                values = jnp.concatenate([lat_value, proj[at, head(h, 2)]], 0)
                prob = softmax(query, keys)
                rounded = prob.astype(BF)
                mixed[at, pl.ds(h * HD, HD)] = dg(rounded, values, 1, 0).astype(BF)
                upstream = gmix[at, pl.ds(h * HD, HD)]
                score = score_grad(prob, upstream, values)
                grads[at, head(h, 0)] = dg(score, keys, 1, 0).astype(BF)
                grad_key = dg(score, query, 0, 0)
                grad_value = dg(rounded, upstream, 0, 0)
                grads[at, head(h, 1)] = grad_key[lats:].astype(BF)
                grads[at, head(h, 2)] = grad_value[lats:].astype(BF)
                key_sum = key_sum + grad_key[:lats]
                value_sum = value_sum + grad_value[:lats]
            lat_grad[:, pl.ds(h * 2 * HD, HD)] = key_sum.astype(BF)
            lat_grad[:, pl.ds(h * 2 * HD + HD, HD)] = value_sum.astype(BF)
        total = dg(lat_grad[:, pl.ds(0, 2 * HD)], qfull[:, pair(0)], 1, 1)
        for h in range(1, heads):
            total = total + dg(lat_grad[:, pl.ds(h * 2 * HD, 2 * HD)], qfull[:, pair(h)], 1, 1)
        part[...] = total.astype(BF)
        grad = summed().astype(BF).astype(F32)
        back, gain_term = norm_back(zfull[mine].astype(F32), gain[...], grad)
        own[...] = back.astype(BF)
        gain_lat[...] = gain_term
        across(dz).start()
        opart[...] = dg(mixed[...], cfull[...], 0, 0).astype(BF)
        lat_t[...] = lat_norm[...].T


    def shard_at(d, s):
        return ring_index((pos + 2 * n - 1 - s) % n if d == 0 else (pos + 1 + s) % n, n)

    def q_copy(src, d, s, h):
        return remote(src, qbuf.at[d, s, h], qsend.at[d, s, h], qrecv.at[d, s, h], dp=hop[d])

    def o_copy(src, d, s, k):
        return remote(src, obuf.at[d, s, k], osend.at[d, s, k], orecv.at[d, s, k], dp=hop[d])

    def o_first(d, k):
        return o_copy(opart.at[o_rows_of(shard_at(d, 0), d, k)], d, 0, k)

    for k in range(pieces):
        for d in range(2):
            @pl.when(shard_at(d, 0) // per == r)
            def _():
                o_first(d, k).start()

    def own_term(shard, d, h):
        at = rows_at(shard * q_rows + d * side, side)
        qpart[d, h] = dg(norm_t[at], grads[:, pl.ds(h * wide_head, wide_head)], 1, 0)

        @pl.when(section == 1)
        def _():
            lat = dg(lat_t[at], lat_grad[:, pl.ds(h * 2 * HD, 2 * HD)], 1, 0)
            qpart[d, h, :, pl.ds(HD, 2 * HD)] += lat

    @pl.when(section == 0)
    def _():
        gmix[pl.ds(0, lats)] = dg(dz[...], ofull[...], 1, 1).astype(BF)

    for h in range(heads):
        @pl.when(section == 0)
        def _():
            prob = enc_prob[pl.ds(h * lats, lats)]
            upstream = gmix[pl.ds(0, lats), pl.ds(h * HD, HD)]
            query = jnp.concatenate(
                [proj[pl.ds(v * rows + half, half), head(h, 0)] for v in range(count)], 0
            )
            score = score_grad(prob, upstream, proj[:, head(h, 2)])
            grad_query = dg(score, proj[:, head(h, 1)], 1, 0).astype(BF)
            for v in range(count):
                grads[pl.ds(v * rows, half), head(h, 0)] = jnp.zeros((half, HD), BF)
                grads[pl.ds(v * rows + half, half), head(h, 0)] = (
                    grad_query[v * half : (v + 1) * half]
                )
            grads[:, head(h, 1)] = dg(score, query, 0, 0).astype(BF)
            grads[:, head(h, 2)] = dg(prob.astype(BF), upstream, 0, 0).astype(BF)

        for d in range(2):
            own_term(shard_at(d, 0), d, h)
            qbuf[d, n - 1, h] = qpart[d, h].astype(BF)
            q_copy(qbuf.at[d, n - 1, h], d, 0, h).start()

    dpart[...] = dg(grads[...], qfull[...], 1, 1).astype(BF)

    def block(j):
        peer = (r + j) % count
        return remote(dpart.at[rows_at(peer * rows, rows)], dbuf.at[j - 1],
                      dsend.at[j - 1], drecv.at[j - 1], render=peer)

    for j in range(1, count):
        block(j).start()
    total = dpart[rows_at(r * rows, rows)].astype(F32)
    for j in range(1, count):
        block(j).wait_recv()
        total = total + dbuf[j - 1].astype(F32)
    back, gain_term = norm_back(tok[...].astype(F32), gain[...], total.astype(BF).astype(F32))
    own_gain[...] = gain_lat[...] + gain_term

    @pl.when(section == 0)
    def _():
        tout[pl.ds(0, half)] = back[:half].astype(BF)
        tout[pl.ds(half, half)] = (back[half:] + dz[mine].astype(F32)).astype(BF)

    @pl.when(section == 1)
    def _():
        tout[...] = (back + cot[...].astype(F32)).astype(BF)

    def gain_copy(j, sender):
        other = (flat + j) % everyone
        return remote(own_gain, gbuf.at[sender], gsend.at[j], grecv.at[j],
                      dp=other // count, render=other % count)

    @pl.loop(1, everyone)
    def _(j):
        gain_copy(j, flat).start()

    @pl.loop(1, n - 1)
    def _(s):
        for h in range(heads):
            for d in range(2):
                own_term(shard_at(d, s), d, h)
        for h in range(heads):
            for d in range(2):
                held = qbuf.at[d, s - 1, h]
                q_copy(held, d, s - 1, h).wait_recv()
                held[...] = (held[...].astype(F32) + qpart[d, h]).astype(BF)
                q_copy(held, d, s, h).start()
        for k in range(pieces):
            for d in range(2):
                shard = shard_at(d, s)

                @pl.when(shard // per == r)
                def _():
                    held = obuf.at[d, s - 1, k]
                    o_copy(held, d, s - 1, k).wait_recv()
                    held[...] = (
                        held[...].astype(F32) + opart[o_rows_of(shard, d, k)].astype(F32)
                    ).astype(BF)
                    o_copy(held, d, s, k).start()

    def q_final(j, d, h, sender):
        ref = qout.at[sender, pl.ds(d * side, side), pl.ds(h * wide_head, wide_head)]
        return remote(ref, ref, esend.at[j - 1, d, h], erecv.at[j - 1, d, h],
                      render=(r + j) % count)

    def o_final(j, d, k):
        ref = oout.at[pl.ds((d * pieces + k) * orr, orr)]
        return remote(ref, ref, hsend.at[j - 1, d, k], hrecv.at[d, k], render=(r + j) % count)

    for h in range(heads):
        for d in range(2):
            own_term(me, d, h)

    gbuf[flat] = own_gain[...]

    @pl.loop(1, everyone)
    def _(j):
        gain_copy(j, (flat + everyone - j) % everyone).wait_recv()
        gain_copy(j, flat).wait_send()

    gout[...] = jnp.sum(gbuf[...], axis=0)

    for h in range(heads):
        for d in range(2):
            held = qbuf.at[d, n - 2, h]
            q_copy(held, d, n - 2, h).wait_recv()
            qout[r, pl.ds(d * side, side), pl.ds(h * wide_head, wide_head)] = (
                held[...].astype(F32) + qpart[d, h]
            ).astype(BF)
            for j in range(1, count):
                q_final(j, d, h, r).start()

    for k in range(pieces):
        for d in range(2):
            @pl.when(own_out)
            def _():
                held = obuf.at[d, n - 2, k]
                o_copy(held, d, n - 2, k).wait_recv()
                oout[pl.ds((d * pieces + k) * orr, orr)] = (
                    held[...].astype(F32) + opart[o_rows_of(me, d, k)].astype(F32)
                ).astype(BF)
                for j in range(1, count):
                    o_final(j, d, k).start()


    @pl.loop(0, n - 1)
    def _(s):
        for d in range(2):
            for h in range(heads):
                q_copy(qbuf.at[d, s, h], d, s, h).wait_send()
            for k in range(pieces):
                q_on(d, s, k).wait_send()

                @pl.when(origin(d, s) // per == r)
                def _():
                    o_on(d, s, k).wait_send()

                @pl.when(shard_at(d, s) // per == r)
                def _():
                    o_copy(obuf.at[d, s, k], d, s, k).wait_send()

    across(dz).wait_send()
    for j in range(1, count):
        for c in token_copies(j, r):
            c.wait_send()
        partial(j).wait_send()
        block(j).wait_send()
        for d in range(2):
            for h in range(heads):
                q_final(j, d, h, r).wait_send()
                q_final(j, d, h, (r + count - j) % count).wait_recv()
            for k in range(pieces):
                @pl.when(own_out)
                def _():
                    o_final(j, d, k).wait_send()

    @pl.when(jnp.logical_not(own_out))
    def _():
        for k in range(pieces):
            for d in range(2):
                o_final(1, d, k).wait_recv()


def whole_step(qw, ow, tok, cot, gain):
    n, count = dims()
    q_rows, wide = qw.shape
    o_rows, depth = ow.shape
    width = wide // 3
    heads = width // HD
    pieces = pieces_of(o_rows)
    orr = o_rows // (2 * pieces)
    rows = tok.shape[0]
    half = rows // 2
    lats = half * count
    scene = rows * count
    everyone = n * count
    sem = lambda *shape: pltpu.SemaphoreType.DMA(shape)
    one = pltpu.SemaphoreType.DMA
    mem = lambda *shape, t=BF: pltpu.VMEM(shape, t)
    ring = (2, n - 1, pieces)
    turn = (2, n - 1, heads)
    return call(
        functools.partial(step_kernel, n, count, width), 0,
        (jax.ShapeDtypeStruct((count, q_rows, wide), BF),
         jax.ShapeDtypeStruct((o_rows, depth), BF),
         jax.ShapeDtypeStruct(tok.shape, BF),
         jax.ShapeDtypeStruct(gain.shape, F32)),
        [VMEM] * 5, (VMEM,) * 4,
        [mem(depth, wide), mem(width, depth), mem(scene, depth), mem(scene, depth),
         mem(depth, scene), mem(scene, wide, t=F32), mem(scene, wide),
         mem(heads * lats, scene, t=F32), mem(scene, width), mem(scene, width),
         mem(lats, depth), mem(depth, lats), mem(lats, 2 * width), mem(lats, 2 * width),
         mem(scene, wide), mem(lats, depth), mem(lats, depth), mem(lats, depth),
         mem(half, depth), mem(count - 1, half, depth), mem(1, depth, t=F32),
         mem(2, heads, q_rows // 2, 3 * HD, t=F32), mem(width, depth), mem(scene, depth),
         mem(2, n, heads, q_rows // 2, 3 * HD), mem(*ring, orr, depth),
         mem(count - 1, rows, depth), mem(everyone, 1, depth, t=F32), mem(1, depth, t=F32),
         sem(*ring), sem(*ring), sem(*ring), sem(*ring),
         sem(2, count - 1), sem(2, count - 1), sem(count - 1), sem(count - 1),
         one, one, sem(count - 1), sem(count - 1),
         sem(*turn), sem(*turn), sem(*ring), sem(*ring),
         sem(count - 1), sem(count - 1), sem(everyone), sem(everyone),
         sem(count - 1, 2, heads), sem(count - 1, 2, heads),
         sem(count - 1, 2, pieces), sem(2, pieces)],
        60, (qw, ow, tok, cot, gain),
    )


def widen_kernel(q_ref, o_ref, qout, oout):
    count, _, wide = q_ref.shape
    width = wide // 3
    for c in range(count):
        for strip in range(3):
            for h in range(width // HD):
                qout[0, :, pl.ds((strip * count + c) * width + h * HD, HD)] = (
                    q_ref[c, :, pl.ds((3 * h + strip) * HD, HD)].astype(F32)
                )
    oout[0] = o_ref[...].astype(F32)


def widen(qsum, osum):
    count, q_rows, wide = qsum.shape
    o_rows, depth = osum.shape
    steps = 4
    qb, ob = q_rows // steps, o_rows // steps
    return pl.pallas_call(
        widen_kernel,
        grid=(steps,),
        out_shape=(jax.ShapeDtypeStruct((1, q_rows, count * wide), F32),
                   jax.ShapeDtypeStruct((1, o_rows, depth), F32)),
        in_specs=[pl.BlockSpec((count, qb, wide), lambda i: (0, i, 0)),
                  pl.BlockSpec((ob, depth), lambda i: (i, 0))],
        out_specs=(pl.BlockSpec((1, qb, count * wide), lambda i: (0, i, 0)),
                   pl.BlockSpec((1, ob, depth), lambda i: (0, i, 0))),
    )(qsum, osum)


def shards(section_tokens, w_qkv, w_out, gains, cotangent):
    n, count = dims()
    width = HEADS * HD // count
    r = lax.axis_index("render")
    qw = jnp.concatenate(
        [lax.dynamic_slice_in_dim(w_qkv[0], (strip * count + r) * width + h * HD, HD, 1)
         for h in range(width // HD) for strip in range(3)], 1
    )
    qsum, osum, token_grad, gain_grad = whole_step(
        qw, w_out[0], section_tokens[0, 0], cotangent[0], gains
    )
    qkv_grad, out_grad = widen(qsum, osum)
    return token_grad[None, None], qkv_grad, out_grad, gain_grad


def solution(mesh):
    in_specs = (
        P("section", "dp", "render", None),
        P("section", "dp", None),
        P("section", "dp", None),
        P("section", None),
        P("dp", "render", None),
    )
    out_specs = (
        P("section", "dp", "render", None),
        P("section", "dp", None),
        P("section", "dp", None),
        P("section", None),
    )
    return jax.shard_map(shards, mesh=mesh, in_specs=in_specs, out_specs=out_specs, check_vma=False)
```

time: 243 us -> 227 us (0.934)
  Pallas kernels: 219 us -> 213 us
  matrix products: 5.16 us -> 0 us
  other arithmetic: 3.05 us -> 0 us
  local copies, waits for them, and re-layouts: 15.1 us -> 12.6 us
    pallas_call x3 -> x1, Pallas kernels: 215 us -> 209 us  [call(): pl.pallas_call(body, out_shape=outs, in_specs=in_specs, out_specs=out_spe...]
    dot_general x1 -> x0, matrix products: 5.16 us -> none  [shards(): proj = jnp.dot(normed, qfull, preferred_element_type=F32).astype(BF)]
    unnamed x46 -> x19, local copies, waits for them, and re-layouts: 12.5 us -> 11.8 us
where the time goes in v3:
time: 227 us; the launch traced here: 226 us
  Pallas kernels  213 us (94%)
  local copies, waits for them, and re-layouts  12.6 us (6%)
    pallas_call x1, Pallas kernels, call(): pl.pallas_call(body, out_shape=outs, in_specs=in_specs, out_specs=out_spe...  209 us
    unnamed x19, local copies, waits for them, and re-layouts  11.8 us

profile of v3, /device:TPU:0, one launch (start us, length us, event | category | flops | bytes accessed | tf_op | source)
XLA Modules:
  0.0 226.2 jit_solution(13276097747445300892)
XLA Ops:
  0.6 0.9 bitcast_dynamic-update-slice_fusion.11
  1.5 0.9 bitcast_dynamic-update-slice_fusion.10
  2.4 0.9 bitcast_dynamic-update-slice_fusion.9
  3.2 0.9 bitcast_dynamic-update-slice_fusion.8
  4.1 0.9 bitcast_dynamic-update-slice_fusion.7
  5.0 0.9 bitcast_dynamic-update-slice_fusion.6
  5.8 0.9 bitcast_dynamic-update-slice_fusion.5
  6.7 0.9 bitcast_dynamic-update-slice_fusion.4
  7.6 0.9 bitcast_dynamic-update-slice_fusion.3
  8.4 0.9 bitcast_dynamic-update-slice_fusion.2
  9.3 0.9 bitcast_dynamic-update-slice_fusion.1
  10.2 0.9 bitcast_dynamic-update-slice_fusion.qw
  11.1 0.0 copy-start
  11.1 0.9 copy-done
  11.9 208.7 %shard_map.84 = (bf16[2,256,1536]{2,1,0:T(8,128)(2,1)}, bf16[128,2048]{1,0:T(8,128)(2,1)}, bf16[128,2048]{1,0:T(8,128)(2,1)}, f32[1,2048]{1,0:T(1,128)}) custom-call(bf16[256,1536]{1,0:T(8,128)(2,1)} %copy-done, bf16[128,2048]{1,0:T(8,128)(2,1)} %bitcast.29, bf16[128,2048]{1,0:T(8,128)(2,1)} %bitcast.30, bf16[128,2048]{1,0:T(8,128)(2,1)} %bitcast.31, ...), custom_call_target="tpu_custom_call" | custom-call | tf_op jit(solution)/shard_map/pallas_call | solution.py:54
  220.6 0.0 copy-start.1
  220.6 0.0 copy-start.2
  220.6 4.2 %shard_map.85 = (f32[1,256,3072]{2,1,0:T(8,128)}, f32[1,128,2048]{2,1,0:T(8,128)}) custom-call(bf16[2,256,1536]{2,1,0:T(8,128)(2,1)} %get-tuple-element.11.q_ref, bf16[128,2048]{1,0:T(8,128)(2,1)} %get-tuple-element.12.o_ref), custom_call_target="tpu_custom_call" | custom-call | tf_op jit(solution)/shard_map/pallas_call | solution.py:613
  224.8 0.0 copy-done.1
  224.8 0.8 copy.22
  225.6 0.0 copy-done.2
  225.6 0.6 copy.23
Async XLA Ops:
  11.1 0.9 copy-start
  220.6 4.2 %copy-start.1 = (bf16[128,2048]{1,0:T(8,128)(2,1)S(1)}, bf16[128,2048]{1,0:T(8,128)(2,1)}, u32[]{:S(2)}) copy-start(bf16[128,2048]{1,0:T(8,128)(2,1)} %get-tuple-element.10) | copy-start | bytes 1572868
  220.6 5.0 %copy-start.2 = (f32[1,2048]{1,0:T(1,128)S(1)}, f32[1,2048]{1,0:T(1,128)}, u32[]{:S(2)}) copy-start(f32[1,2048]{1,0:T(1,128)} %get-tuple-element.23) | copy-start | bytes 24580

commit v4 on v3

--- a/solution.py
+++ b/solution.py
@@ -93,11 +93,11 @@
     return back, jnp.sum(grad * wide * scale, axis=0, keepdims=True)
 
 
-def step_kernel(n, count, width, qw, ow, tok, cot, gain,
+def step_kernel(n, count, width, w, ow, tok, cot, gain,
                 qout, oout, tout, gout,
                 qfull, ofull, tfull, cfull, norm_t, acc, proj, enc_prob, mixed, gmix,
                 lat_norm, lat_t, lat_kv, lat_grad, grads, zfull, dz, part, own, got, gain_lat,
-                qpart, opart, dpart, qbuf, obuf, dbuf, gbuf, own_gain,
+                qpart, opart, dpart, qbuf, obuf, dbuf, gbuf, own_gain, wsem,
                 gqs, gqr, gos, gor, tsend, trecv, psend, precv, xsend, xrecv, fsend, frecv,
                 qsend, qrecv, osend, orecv, dsend, drecv, gsend, grecv, esend, erecv, hsend, hrecv):
     me = lax.axis_index("dp")
@@ -106,7 +106,7 @@
     pos = ring_position(me, n)
     hop = [ring_index((pos + 1) % n, n), ring_index((pos + n - 1) % n, n)]
     per = n // count
-    q_rows, o_rows = qw.shape[0], ow.shape[0]
+    q_rows, o_rows = w.shape[0], ow.shape[0]
     pieces = pieces_of(o_rows)
     qr, orr = q_rows // (2 * pieces), o_rows // (2 * pieces)
     side = q_rows // 2
@@ -121,6 +121,18 @@
     mine = rows_at(r * half, half)
     barrier = pltpu.get_barrier_semaphore()
 
+    def columns(h, strip):
+        start = pl.multiple_of((strip * count + r) * width + h * HD, HD)
+        return pltpu.make_async_copy(
+            w.at[:, pl.ds(start, HD)],
+            qfull.at[rows_at(me * q_rows, q_rows), pl.ds(h * 3 * HD + strip * HD, HD)],
+            wsem.at[h, strip],
+        )
+
+    strips = [columns(h, strip) for h in range(heads) for strip in range(3)]
+    for c in strips:
+        c.start()
+
     @pl.loop(1, everyone)
     def _(j):
         other = (flat + j) % everyone
@@ -155,13 +167,15 @@
             c.start()
 
     def first_q(d, k):
-        return remote(qw.at[pl.ds((d * pieces + k) * qr, qr)], q_at(me, d, k),
+        return remote(q_at(me, d, k), q_at(me, d, k),
                       gqs.at[d, 0, k], gqr.at[d, 0, k], dp=hop[d])
 
     def first_o(d, k):
         return remote(ow.at[pl.ds((d * pieces + k) * orr, orr)], ofull.at[o_rows_of(me, d, k)],
                       gos.at[d, 0, k], gor.at[d, 0, k], dp=hop[d])
 
+    for c in strips:
+        c.wait()
     for k in range(pieces):
         for d in range(2):
             first_q(d, k).start()
@@ -211,8 +225,6 @@
         for d in range(2):
             at = rows_at(origin(d, s) * q_rows + d * side, side)
             acc[...] += dg(norm_t[at], qfull[at], 0, 0)
-
-    qfull[rows_at(me * q_rows, q_rows)] = qw[...]
 
     @pl.when(own_out)
     def _():
@@ -548,9 +560,9 @@
                 o_final(1, d, k).wait_recv()
 
 
-def whole_step(qw, ow, tok, cot, gain):
+def whole_step(w, ow, tok, cot, gain):
     n, count = dims()
-    q_rows, wide = qw.shape
+    q_rows, wide = w.shape[0], w.shape[1] // count
     o_rows, depth = ow.shape
     width = wide // 3
     heads = width // HD
@@ -572,7 +584,7 @@
          jax.ShapeDtypeStruct((o_rows, depth), BF),
          jax.ShapeDtypeStruct(tok.shape, BF),
          jax.ShapeDtypeStruct(gain.shape, F32)),
-        [VMEM] * 5, (VMEM,) * 4,
+        [ANY] + [VMEM] * 4, (VMEM,) * 4,
         [mem(depth, wide), mem(width, depth), mem(scene, depth), mem(scene, depth),
          mem(depth, scene), mem(scene, wide, t=F32), mem(scene, wide),
          mem(heads * lats, scene, t=F32), mem(scene, width), mem(scene, width),
@@ -581,7 +593,7 @@
          mem(half, depth), mem(count - 1, half, depth), mem(1, depth, t=F32),
          mem(2, heads, q_rows // 2, 3 * HD, t=F32), mem(width, depth), mem(scene, depth),
          mem(2, n, heads, q_rows // 2, 3 * HD), mem(*ring, orr, depth),
-         mem(count - 1, rows, depth), mem(everyone, 1, depth, t=F32), mem(1, depth, t=F32),
+         mem(count - 1, rows, depth), mem(everyone, 1, depth, t=F32), mem(1, depth, t=F32), sem(heads, 3),
          sem(*ring), sem(*ring), sem(*ring), sem(*ring),
          sem(2, count - 1), sem(2, count - 1), sem(count - 1), sem(count - 1),
          one, one, sem(count - 1), sem(count - 1),
@@ -589,7 +601,7 @@
          sem(count - 1), sem(count - 1), sem(everyone), sem(everyone),
          sem(count - 1, 2, heads), sem(count - 1, 2, heads),
          sem(count - 1, 2, pieces), sem(2, pieces)],
-        60, (qw, ow, tok, cot, gain),
+        60, (w, ow, tok, cot, gain),
     )
 
 
@@ -623,15 +635,8 @@
 
 
 def shards(section_tokens, w_qkv, w_out, gains, cotangent):
-    n, count = dims()
-    width = HEADS * HD // count
-    r = lax.axis_index("render")
-    qw = jnp.concatenate(
-        [lax.dynamic_slice_in_dim(w_qkv[0], (strip * count + r) * width + h * HD, HD, 1)
-         for h in range(width // HD) for strip in range(3)], 1
-    )
     qsum, osum, token_grad, gain_grad = whole_step(
-        qw, w_out[0], section_tokens[0, 0], cotangent[0], gains
+        w_qkv[0], w_out[0], section_tokens[0, 0], cotangent[0], gains
     )
     qkv_grad, out_grad = widen(qsum, osum)
     return token_grad[None, None], qkv_grad, out_grad, gain_grad

time: 227 us -> 215 us (0.947)
  local copies, waits for them, and re-layouts: 12.6 us -> 1.4 us
    unnamed x19 -> x6, local copies, waits for them, and re-layouts: 11.8 us -> 1.4 us
where the time goes in v4:
time: 215 us
  Pallas kernels  213 us (99%)
    pallas_call x1, Pallas kernels, call(): pl.pallas_call(body, out_shape=outs, in_specs=in_specs, out_specs=out_spe...  209 us

profile of v4, /device:TPU:0, one launch (start us, length us, event | category | flops | bytes accessed | tf_op | source)
XLA Modules:
  0.0 214.8 jit_solution(8020704525215995955)
XLA Ops:
  0.6 208.6 %shard_map.84 = (bf16[2,256,1536]{2,1,0:T(8,128)(2,1)}, bf16[128,2048]{1,0:T(8,128)(2,1)}, bf16[128,2048]{1,0:T(8,128)(2,1)}, f32[1,2048]{1,0:T(1,128)}) custom-call(bf16[256,3072]{1,0:T(8,128)(2,1)} %bitcast.5, bf16[128,2048]{1,0:T(8,128)(2,1)} %bitcast.7, bf16[128,2048]{1,0:T(8,128)(2,1)} %bitcast.8, bf16[128,2048]{1,0:T(8,128)(2,1)} %bitcast.9, ...), custom_call_target="tpu_custom_call" | custom-call | tf_op jit(solution)/shard_map/pallas_call | solution.py:54
  209.2 0.0 copy-start
  209.2 0.0 copy-start.1
  209.2 4.2 %shard_map.85 = (f32[1,256,3072]{2,1,0:T(8,128)}, f32[1,128,2048]{2,1,0:T(8,128)}) custom-call(bf16[2,256,1536]{2,1,0:T(8,128)(2,1)} %get-tuple-element.11.q_ref, bf16[128,2048]{1,0:T(8,128)(2,1)} %get-tuple-element.12.o_ref), custom_call_target="tpu_custom_call" | custom-call | tf_op jit(solution)/shard_map/pallas_call | solution.py:625
  213.4 0.0 copy-done
  213.4 0.8 copy.11
  214.2 0.0 copy-done.1
  214.2 0.6 copy.12
Async XLA Ops:
  209.2 4.2 %copy-start = (bf16[128,2048]{1,0:T(8,128)(2,1)S(1)}, bf16[128,2048]{1,0:T(8,128)(2,1)}, u32[]{:S(2)}) copy-start(bf16[128,2048]{1,0:T(8,128)(2,1)} %get-tuple-element.10) | copy-start | bytes 1572868
  209.2 5.0 %copy-start.1 = (f32[1,2048]{1,0:T(1,128)S(1)}, f32[1,2048]{1,0:T(1,128)}, u32[]{:S(2)}) copy-start(f32[1,2048]{1,0:T(1,128)} %get-tuple-element.23) | copy-start | bytes 24580
